TPU v7x, 768 devices: a whole 4x8x12 slice. The times are simulated.
768 devices in a mesh: ctx: 96 (over z, y), head: 8 (over x, core).
Axes of the slice: x: 4, y: 8, z: 12, core: 2. Of those that a mesh axis runs over, the one named last changes fastest.
Arguments:
- queries: bfloat16 [12288, 3072], P('ctx', 'head'), may hold values from -6 to 6
- key_vectors: bfloat16 [12288, 3072], P('ctx', 'head'), may hold values from -6 to 6
- value_vectors: bfloat16 [12288, 3072], P('ctx', 'head'), may hold values from -13 to 13
- out_grad: bfloat16 [12288, 3072], P('ctx', 'head'), may hold values from -6 to 6
- log_decay: float32 [32, 12288], P('head', 'ctx'), may hold values from -2 to 0, as said below
- doc_ids: int32 [12288], replicated, may hold values from 0 to 5, never falling along the last dimension, each value on 1 to 4096 neighbouring positions
Outputs:
- attended: bfloat16 [12288, 3072], P('ctx', 'head')
- grad_query: bfloat16 [12288, 3072], P('ctx', 'head')
- grad_key: bfloat16 [12288, 3072], P('ctx', 'head')
- grad_value: bfloat16 [12288, 3072], P('ctx', 'head')
Inputs may be any that keep to these rules, and one draw needn't show every extreme that they name: `doc_ids`: ids never fall; each of the 6 documents holds 1 to 4096 tokens, and one holds exactly that many. `log_decay`: strictly negative.
All inputs are finite; a program needn't handle non-finite values.
Results may differ from a plain program's by a relative error of at most 0.0014.
Values sent between devices are 32-bit elements; how exact they have to be, the bound alone decides.
A program may use at most 64 MiB of HBM per device.

v0:
```python
import jax
import jax.numpy as jnp
from jax import lax
from jax.sharding import PartitionSpec as P

HEAD_TOTAL = 32
DH = 96
BLOCK = 128


highest = lax.Precision.HIGHEST
epsilon = 1e-05


def carried_in(part, axis, combine, identity, reverse):
    count = lax.axis_size(axis)
    place = lax.axis_index(axis)
    ahead = count - 1 - place if reverse else place
    gathered = jax.tree.map(lambda a: lax.all_gather(a, axis), part)
    state = jax.tree.map(lambda a, e: jnp.zeros_like(a) + jnp.asarray(e, a.dtype), part, identity)

    def one(step, state):
        source = count - 1 - step if reverse else step
        return combine(
            state, jax.tree.map(lambda a: lax.dynamic_index_in_dim(a, source, 0, False), gathered)
        )

    return lax.fori_loop(0, ahead, one, state)


def contract(pattern, operand_one, operand_two):
    return jnp.einsum(pattern, operand_one, operand_two, precision=highest)


def block_weights(log_rates, doc_block, before):
    cumulative = jnp.cumsum(log_rates, axis=1)
    spread = cumulative[:, :, None] - cumulative[:, None, :]
    length = doc_block.shape[0]
    row_index = lax.broadcasted_iota(jnp.int32, (length, length), 0)
    col_index = lax.broadcasted_iota(jnp.int32, (length, length), 1)
    inside = (row_index >= col_index) & (doc_block[:, None] == doc_block[None, :])
    within = jnp.exp(jnp.minimum(spread, 0.0)) * inside.astype(jnp.float32)[None]
    carried = (doc_block == before).astype(jnp.float32)
    entering = jnp.exp(cumulative) * carried[None, :]
    final_sum = cumulative[:, -1:]
    leaving = (
        jnp.exp(final_sum - cumulative) * (doc_block == doc_block[-1]).astype(jnp.float32)[None, :]
    )
    passing = jnp.exp(final_sum[:, 0]) * carried[-1]
    return (within, entering, leaving, passing)


def block_forward(scaled, key_now, value_now, carry_state, weights):
    within, entering, leaving, passing = weights
    scores = contract("thd,shd->hts", scaled, key_now)
    local_part = contract("hts,shd->thd", within * scores, value_now)
    carried = contract("thd,hde->the", scaled, carry_state) * entering.T[:, :, None]
    update = contract("shd,she->hde", key_now * leaving.T[:, :, None], value_now)
    return (local_part + carried, passing[:, None, None] * carry_state + update)


def block_backward(scaled, key_now, value_now, grad_now, state_in, grad_state, weights):
    within, entering, leaving, passing = weights
    scores = contract("thd,shd->hts", scaled, key_now)
    masked_back = within * contract("thd,shd->hts", grad_now, value_now)
    grad_entry = grad_now * entering.T[:, :, None]
    grad_scaled = contract("hts,shd->thd", masked_back, key_now) + contract(
        "the,hde->thd", grad_entry, state_in
    )
    grad_keys = (
        contract("hts,thd->shd", masked_back, scaled)
        + contract("she,hde->shd", value_now, grad_state) * leaving.T[:, :, None]
    )
    grad_values = (
        contract("hts,thd->shd", within * scores, grad_now)
        + contract("shd,hde->she", key_now, grad_state) * leaving.T[:, :, None]
    )
    grad_in = passing[:, None, None] * grad_state + contract("thd,the->hde", scaled, grad_entry)
    return (grad_scaled, grad_keys, grad_values, grad_in)


def combine(earlier, latter):
    return (earlier[0] * latter[0], latter[0][:, None] * earlier[1] + latter[1])


def local(queries, key_vectors, value_vectors, out_grad, log_decay, doc_ids):
    head_count = log_decay.shape[0]
    tokens = log_decay.shape[1]
    blocks = tokens // BLOCK
    factor = DH ** (-0.5)
    full_width = HEAD_TOTAL * DH

    def unfold(rows_in):
        return rows_in.astype(jnp.float32).reshape(tokens, head_count, DH)

    scaled = unfold(queries) * factor
    key_all = unfold(key_vectors)
    value_all = unfold(value_vectors)
    first_token = lax.axis_index("ctx") * tokens
    doc_local = lax.dynamic_slice_in_dim(doc_ids, first_token, tokens)
    previous = lax.dynamic_slice_in_dim(doc_ids, jnp.maximum(first_token - 1, 0), 1)[0]
    previous = jnp.where(first_token > 0, previous, -1)
    carry_state = jnp.zeros((head_count, DH, DH), jnp.float32)
    prefix = jnp.ones((head_count,), jnp.float32)
    number = 0
    weights = block_weights(log_decay, doc_local, previous)
    weight_list = [weights]
    state_list = [carry_state]
    prefix_list = [prefix]
    out_now, carry_state = block_forward(scaled, key_all, value_all, carry_state, weights)
    prefix = prefix * weights[3]
    identity = (jnp.ones((head_count,), jnp.float32), jnp.zeros((head_count, DH * DH), jnp.float32))
    state_pair = (prefix, carry_state.reshape(head_count, DH * DH))
    arriving_flat = carried_in(state_pair, "ctx", combine, identity, False)[1]
    arriving = arriving_flat.reshape(head_count, DH, DH)
    entry_weights = weight_list[0][1] * prefix_list[0][:, None]
    attended_raw = (
        out_now + contract("thd,hde->the", scaled, arriving) * entry_weights.T[:, :, None]
    )
    local_squares = jnp.sum(attended_raw * attended_raw, axis=(1, 2))
    total_squares = lax.psum(local_squares, "head")
    rscale = lax.rsqrt(total_squares / full_width + epsilon)
    normed = attended_raw * rscale[:, None, None]
    attended = normed.reshape(tokens, head_count * DH).astype(jnp.bfloat16)
    grad_in = unfold(out_grad)
    local_dot = jnp.sum(grad_in * attended_raw, axis=(1, 2))
    total_dot = lax.psum(local_dot, "head")
    drift = rscale * rscale * rscale * total_dot / full_width
    grad_out = rscale[:, None, None] * grad_in - attended_raw * drift[:, None, None]
    grad_state = jnp.zeros((head_count, DH, DH), jnp.float32)
    suffix = jnp.ones((head_count,), jnp.float32)
    query_parts = [None] * blocks
    key_parts = [None] * blocks
    value_parts = [None] * blocks
    leave_list = [None] * blocks
    for number in reversed(range(blocks)):
        weights = weight_list[number]
        true_state = state_list[number] + prefix_list[number][:, None, None] * arriving
        part_query, part_key, part_value, grad_state = block_backward(
            scaled, key_all, value_all, grad_out, true_state, grad_state, weights
        )
        query_parts[number] = part_query
        key_parts[number] = part_key
        value_parts[number] = part_value
        leave_list[number] = weights[2] * suffix[:, None]
        suffix = suffix * weights[3]
    grad_pair = (prefix, grad_state.reshape(head_count, DH * DH))
    returned_flat = carried_in(grad_pair, "ctx", combine, identity, True)[1]
    returned = returned_flat.reshape(head_count, DH, DH)
    leave_all = leave_list[0].T[:, :, None]
    grad_keys = key_parts[0] + contract("she,hde->shd", value_all, returned) * leave_all
    grad_values = value_parts[0] + contract("shd,hde->she", key_all, returned) * leave_all
    grad_queries = query_parts[0] * factor

    def fold_rows(source_array):
        return source_array.reshape(tokens, head_count * DH).astype(jnp.bfloat16)

    return (attended, fold_rows(grad_queries), fold_rows(grad_keys), fold_rows(grad_values))


def solution(mesh):
    return jax.shard_map(
        local,
        mesh=mesh,
        in_specs=(
            P("ctx", "head"),
            P("ctx", "head"),
            P("ctx", "head"),
            P("ctx", "head"),
            P("head", "ctx"),
            P(),
        ),
        out_specs=(P("ctx", "head"), P("ctx", "head"), P("ctx", "head"), P("ctx", "head")),
        check_vma=False,
    )
```

profile of v0, /device:TPU:6, one launch (start us, length us, event | category | flops | bytes accessed | tf_op | source)
XLA Modules:
  0.0 625.8 jit_solution(5970611690696459636)
XLA Ops:
  7.2 1.3 dynamic_slice.33
  18.6 1.3 dynamic-slice
  20.8 223.5 %all-reduce = f32[384]{0:T(512)S(1)} all-reduce(f32[384]{0:T(512)S(1)} %dynamic-update-slice), channel_id=2, replica_groups=mesh['ctx'=96,'head'=8] {'ctx'}, use_global_device_ids=true, to_apply=%add | all-reduce | flops 384 | bytes 3072
  247.4 10.0 %all-reduce.1 = (f32[128]{0:T(128)S(1)}, f32[128]{0:T(128)S(1)}) all-reduce(f32[128]{0:T(128)S(1)} %get-tuple-element.147, f32[128]{0:T(128)S(1)} %get-tuple-element.146), channel_id=1, replica_groups=mesh['ctx'=96,'head'=8] {'head'}, use_global_device_ids=true, to_apply=%region_4.5 | all-reduce | flops 256 | bytes 2048 | tf_op jit(solution)/shard_map/psum | solution.py:121
  262.0 250.2 %all-gather.6.cloned.1.call-done = f32[96,4,9216]{2,1,0:T(4,128)} async-done(((f32[1,4,9216]{2,1,0:T(4,128)}), f32[96,4,9216]{2,1,0:T(4,128)}) %all-gather.6.cloned.1.call-update) | async-done | bytes 14155792 | tf_op jit(solution)/shard_map/all_gather | solution.py:19
  512.2 103.7 %while.27 = (s32[]{:T(128)}, f32[4,9216]{1,0:T(4,128)S(1)}, s32[]{:T(128)}, f32[96,4]{1,0:T(8,128)S(1)}, f32[96,4,9216]{2,1,0:T(4,128)}, /*index=5*/s32[]{:T(128)}, s32[]{:T(128)}, s32[]{:T(128)}, s32[]{:T(128)}) while((s32[]{:T(128)}, f32[4,9216]{1,0:T(4,128)S(1)}, s32[]{:T(128)}, f32[96,4]{1,0:T(8,128)S(1)}, f32[96,4,9216]{2,1,0:T(4,128)}, ...), condition=%wide.region_8.9_spmd, body=%wide.region_7.8_spmd.sunk | while | flops 73734 | bytes 442563 | solution.py:28
  517.7 1.1 bitcast_add_fusion.5
  518.8 1.1 bitcast_add_fusion.5
  519.9 1.1 bitcast_add_fusion.5
  521.0 1.1 bitcast_add_fusion.5
  522.1 1.1 bitcast_add_fusion.5
  523.2 1.1 bitcast_add_fusion.5
  524.3 1.1 bitcast_add_fusion.5
  525.4 1.1 bitcast_add_fusion.5
  526.5 1.1 bitcast_add_fusion.5
  527.6 1.1 bitcast_add_fusion.5
  538.5 1.1 bitcast_add_fusion.5
  539.6 1.1 bitcast_add_fusion.5
  540.7 1.1 bitcast_add_fusion.5
  541.8 1.1 bitcast_add_fusion.5
  542.9 1.1 bitcast_add_fusion.5
  543.9 1.1 bitcast_add_fusion.5
  545.0 1.1 bitcast_add_fusion.5
  546.1 1.1 bitcast_add_fusion.5
  547.2 1.1 bitcast_add_fusion.5
  548.3 1.1 bitcast_add_fusion.5
  559.2 1.1 bitcast_add_fusion.5
  560.3 1.1 bitcast_add_fusion.5
  561.4 1.1 bitcast_add_fusion.5
  562.5 1.1 bitcast_add_fusion.5
  563.6 1.1 bitcast_add_fusion.5
  564.7 1.1 bitcast_add_fusion.5
  565.8 1.1 bitcast_add_fusion.5
  566.9 1.1 bitcast_add_fusion.5
  568.0 1.1 bitcast_add_fusion.5
  569.1 1.1 bitcast_add_fusion.5
  580.0 1.1 bitcast_add_fusion.5
  581.1 1.1 bitcast_add_fusion.5
  582.2 1.1 bitcast_add_fusion.5
  583.2 1.1 bitcast_add_fusion.5
  584.3 1.1 bitcast_add_fusion.5
  585.4 1.1 bitcast_add_fusion.5
  586.5 1.1 bitcast_add_fusion.5
  587.6 1.1 bitcast_add_fusion.5
  588.7 1.1 bitcast_add_fusion.5
  589.8 1.1 bitcast_add_fusion.5
  600.7 1.1 bitcast_add_fusion.5
  601.8 1.1 bitcast_add_fusion.5
  (198 shorter events, 77.1 us)
Async XLA Ops:
  7.2 239.5 %all-gather.4.cloned.1.call-start = ((), (), s32[]{:S(2)}) async-start(), calls=%async_computation | async-start | bytes 14303232 | tf_op jit(solution)/shard_map/all_gather | solution.py:19
  17.5 494.7 %all-gather.6.cloned.1.call-start = ((), (), s32[]{:S(2)}) async-start(), calls=%async_computation.1 | async-start | bytes 14303232 | tf_op jit(solution)/shard_map/all_gather | solution.py:19
Sparse Core Ops, SparseCore 0:
  17.7 169.6 all-gather.3
  259.0 253.1 all-gather.5
where the time goes:
time: 628 us; the launch traced here: 626 us
  waiting for transfers between devices  250 us (40%)
  blocking collectives  233 us (37%)
  other arithmetic  104 us (17%)
  between operations  15.6 us (2%)
  local copies, waits for them, and re-layouts  14.1 us (2%)
    all_gather x2, waiting for transfers between devices, carried_in(): gathered = jax.tree.map(lambda a: lax.all_gather(a, axis), part)  250 us
    unnamed x1, blocking collectives  223 us
    add x95, other arithmetic, combine(): return (earlier[0] * latter[0], latter[0][:, None] * earlier[1] + latter[1])  100 us
  transfers between devices with their start and end apart: 2, of which 1 were waited for; matrix products, arithmetic and copies ran while one was open for 1% of the time, Pallas kernels for 0%

commit v1 on v0

v1 whole, which is shorter than its diff:
```python
import jax
import jax.numpy as jnp
from jax import lax
from jax.experimental import pallas as pl
from jax.experimental.pallas import tpu as pltpu
from jax.sharding import PartitionSpec as P

HEADS = 4
DH = 96
TOK = 128
WIDTH = HEADS * DH
FULL = 3072
ROW = 8
ROWS = 12
HEAD_DEVS = 8
HALF = DH // 2
EPS = 1e-05
FACTOR = DH ** (-0.5)
F32 = jnp.float32
BF16 = jnp.bfloat16
MESH = pl.DeviceIdType.MESH


def nn(a, b):
    return lax.dot_general(a, b, (((1,), (0,)), ((), ())), preferred_element_type=F32)


def nt(a, b):
    return lax.dot_general(a, b, (((1,), (1,)), ((), ())), preferred_element_type=F32)


def split(x):
    hi = x.astype(BF16)
    return hi, (x - hi.astype(F32)).astype(BF16)


def two(dot, a, b):
    return dot(a[0], b) + dot(a[1], b)


def two_right(dot, a, b):
    return dot(a, b[0]) + dot(a, b[1])


def three(dot, a, b):
    return dot(a[0], b[0]) + (dot(a[0], b[1]) + dot(a[1], b[0]))


def kernel(
    q_ref, k_ref, v_ref, g_ref, ld_ref, doc_ref,
    att_ref, dq_ref, dk_ref, dv_ref,
    qh, kh, vh, gh, qt, within, score, ent, leave, out, state_hi, state_lo,
    out_hi, out_lo, dkl, dvl,
    up, up_in, part, back, back_in, zout, zin,
    upb, upb_in, partb, backb, backb_in, zoutb, zinb,
    hsend, hrecv,
    a_send, a_recv, z_send, z_recv, h_send, h_recv,
):
    ctx = lax.axis_index("ctx")
    head = lax.axis_index("head")
    y = lax.rem(ctx, ROW)
    z = ctx // ROW

    def at_row(step):
        return lax.rem(z + step + ROWS, ROWS) * ROW + y

    barrier = pltpu.get_barrier_semaphore()
    for step in range(1, ROW):
        pl.semaphore_signal(
            barrier, inc=1, device_id=(z * ROW + lax.rem(y + step, ROW), head), device_id_type=MESH
        )
    for step in (-2, -1, 1, 2):
        pl.semaphore_signal(barrier, inc=1, device_id=(at_row(step), head), device_id_type=MESH)
    for step in range(1, HEAD_DEVS):
        pl.semaphore_signal(
            barrier, inc=1, device_id=(ctx, lax.rem(head + step, HEAD_DEVS)), device_id_type=MESH
        )

    lane = lax.broadcasted_iota(jnp.int32, (TOK, TOK), 1)
    sub = lax.broadcasted_iota(jnp.int32, (TOK, TOK), 0)
    real = lane < DH
    real_half = lax.broadcasted_iota(jnp.int32, (HALF, TOK), 1) < DH

    def heads_of(ref):
        tiles = [ref[:, TOK * t : TOK * t + TOK].astype(F32) for t in range(3)]
        zero = jnp.zeros((TOK, TOK), F32)
        h0 = tiles[0]
        h1 = pltpu.roll(jnp.where(lane >= 96, tiles[0], tiles[1]), 32, 1)
        h2 = pltpu.roll(jnp.where(lane >= 64, tiles[1], tiles[2]), 64, 1)
        h3 = pltpu.roll(tiles[2], 96, 1)
        return [jnp.where(real, h, zero) for h in (h0, h1, h2, h3)]

    def put_heads(ref, parts):
        r1 = pltpu.roll(parts[1], 96, 1)
        r2 = pltpu.roll(parts[2], 64, 1)
        r3 = pltpu.roll(parts[3], 32, 1)
        ref[:, 0:TOK] = jnp.where(lane < 96, parts[0], r1).astype(BF16)
        ref[:, TOK : 2 * TOK] = jnp.where(lane < 64, r1, r2).astype(BF16)
        ref[:, 2 * TOK : 3 * TOK] = jnp.where(lane < 32, r2, r3).astype(BF16)

    def spread(row):
        return jnp.transpose(jnp.broadcast_to(row, (TOK, TOK)))

    upper = (sub <= lane).astype(F32)
    sums = lax.dot_general(
        ld_ref[...], upper, (((1,), (0,)), ((), ())),
        precision=lax.Precision.HIGHEST, preferred_element_type=F32,
    )
    doc_row = doc_ref[pl.ds(ctx, 1), :].astype(F32)
    earlier = doc_ref[pl.ds(jnp.maximum(ctx - 1, 0), 1), :].astype(F32)[:, TOK - 1 : TOK]
    before = jnp.where(ctx > 0, earlier, -1.0)
    last = doc_row[:, TOK - 1 : TOK]
    enter_row = (doc_row == before).astype(F32)
    leave_row = (doc_row == last).astype(F32)
    through = (last == before).astype(F32)
    doc_col = spread(doc_row)
    inside = (sub >= lane) & (doc_col == doc_row)
    enter_col = (doc_col == before).astype(F32)
    leave_col = (doc_col == last).astype(F32)

    k_heads = heads_of(k_ref)
    v_heads = heads_of(v_ref)
    passing = []
    for h in range(HEADS):
        row = sums[h : h + 1, :]
        final = row[:, TOK - 1 : TOK]
        passing.append(jnp.exp(final) * through)
        vb = v_heads[h].astype(BF16)
        vh[h] = vb
        kh[h] = k_heads[h].astype(BF16)
        kt = jnp.transpose(k_heads[h]) * (jnp.exp(final - row) * leave_row)
        update = two(nn, split(kt), vb)
        tile = jnp.where(real, update, passing[h])
        up[2 * h] = tile[0:HALF]
        up[2 * h + 1] = tile[HALF:DH]

    pl.semaphore_wait(barrier, (ROW - 1) + 4 + (HEAD_DEVS - 1))

    def remote(src, dst, send_sem, recv_sem, target):
        return pltpu.make_async_remote_copy(
            src_ref=src, dst_ref=dst, send_sem=send_sem, recv_sem=recv_sem,
            device_id=target, device_id_type=MESH,
        )

    def across(phase, src, dst):
        copies = []
        for step in range(1, ROW):
            other = lax.rem(y + step, ROW)
            copy = remote(
                src.at[other], dst.at[y], a_send.at[phase, step], a_recv.at[phase, y],
                (z * ROW + other, head),
            )
            copy.start()
            copies.append(copy)
        dst[pl.ds(y, 1)] = src[pl.ds(y, 1)]
        return copies

    def arrive(phase, dst):
        for step in range(1, ROW):
            other = lax.rem(y + step, ROW)
            remote(
                dst.at[other], dst.at[other], a_send.at[phase, step], a_recv.at[phase, other],
                (z * ROW + other, head),
            ).wait_recv()

    def factor_of(tile):
        return jnp.broadcast_to(tile[:, DH : DH + 1], tile.shape)

    def join(near, far):
        return jnp.where(real_half, near, 0.0) + factor_of(near) * far

    def row_scan(base, forward, arrived, prefix, zo, zi, result):
        arrive(base, arrived)
        order = range(ROW) if forward else range(ROW - 1, -1, -1)
        running = jnp.where(real_half, 0.0, 1.0)
        for place in order:
            prefix[place] = running
            running = join(arrived[place], running)
        zo[0] = running
        sign = 1 if forward else -1
        sends = []
        for n, (slot, step) in enumerate(((0, sign), (0, 2 * sign))):
            copy = remote(
                zo.at[slot], zi.at[n], z_send.at[base, n], z_recv.at[base, n], (at_row(step), head)
            )
            copy.start()
            sends.append(copy)
        sends[0].wait_recv()
        sends[1].wait_recv()
        pair = join(zi[0], zi[1])
        zo[1] = pair
        copy = remote(
            zo.at[1], zi.at[2], z_send.at[base, 2], z_recv.at[base, 2], (at_row(2 * sign), head)
        )
        copy.start()
        sends.append(copy)
        copy.wait_recv()
        entry = pair + factor_of(pair) * zi[2]
        for place in range(ROW):
            tile = prefix[place]
            result[place] = tile + factor_of(tile) * entry
        return sends

    def state_of(arrived, h):
        tile = jnp.concatenate(
            [arrived[2 * h], arrived[2 * h + 1], jnp.zeros((TOK - DH, TOK), F32)], axis=0
        )
        return jnp.where(real, tile, 0.0)

    pending = across(0, up, up_in)

    q_heads = heads_of(q_ref)
    g_heads = heads_of(g_ref)
    for h in range(HEADS):
        row = sums[h : h + 1, :]
        final = row[:, TOK - 1 : TOK]
        col = spread(row)
        qb = q_heads[h].astype(BF16)
        qh[h] = qb
        gh[h] = g_heads[h].astype(BF16)
        qt[h] = jnp.transpose(q_heads[h]) * (jnp.exp(row) * enter_row * FACTOR)
        ent[h] = jnp.exp(col) * enter_col * FACTOR
        leave[h] = jnp.exp(final - col) * leave_col
        weight = jnp.where(inside, jnp.exp(jnp.minimum(col - row, 0.0)), 0.0)
        within[h] = weight
        scores = weight * (nt(qb, kh[h]) * FACTOR)
        score[h] = scores
        out[h] = two(nn, split(scores), vh[h])

    pending += row_scan(0, True, up_in, part, zout, zin, back)
    pending += across(1, back, back_in)
    arrive(1, back_in)

    squares = jnp.zeros((TOK, TOK), F32)
    dots = jnp.zeros((TOK, TOK), F32)
    for h in range(HEADS):
        pair = split(state_of(back_in, h))
        state_hi[h] = pair[0]
        state_lo[h] = pair[1]
        now = out[h] + ent[h] * two_right(nn, qh[h], pair)
        out[h] = now
        squares = squares + now * now
        dots = dots + now * gh[h].astype(F32)
    square_row = jnp.sum(jnp.transpose(squares), axis=0, keepdims=True)
    dot_row = jnp.sum(jnp.transpose(dots), axis=0, keepdims=True)
    small = lax.broadcasted_iota(jnp.int32, (8, TOK), 0)
    tile = jnp.where(small == 0, square_row, dot_row)
    hsend[...] = tile
    for step in range(1, HEAD_DEVS):
        other = lax.rem(head + step, HEAD_DEVS)
        copy = remote(hsend, hrecv.at[head], h_send.at[step], h_recv.at[head], (ctx, other))
        copy.start()
        pending.append(copy)
    hrecv[pl.ds(head, 1)] = tile[None]
    for h in range(HEADS):
        pair = split(out[h])
        out_hi[h] = pair[0]
        out_lo[h] = pair[1]
    for step in range(1, HEAD_DEVS):
        other = lax.rem(head + step, HEAD_DEVS)
        remote(
            hrecv.at[other], hrecv.at[other], h_send.at[step], h_recv.at[other], (ctx, other)
        ).wait_recv()
    total = hrecv[0]
    for slot in range(1, HEAD_DEVS):
        total = total + hrecv[slot]
    rscale = lax.rsqrt(total[0:1] / FULL + EPS)
    drift = rscale * rscale * rscale * total[1:2] / FULL

    for h in range(HEADS):
        near = split(qt[h] * rscale)
        far = split(qt[h] * drift)
        pulled = two(nn, near, gh[h]) - three(nn, far, (out_hi[h], out_lo[h]))
        tile = jnp.where(real, pulled, passing[h])
        upb[2 * h] = tile[0:HALF]
        upb[2 * h + 1] = tile[HALF:DH]

    pending += across(2, upb, upb_in)

    rscale_col = spread(rscale)
    drift_col = spread(drift)
    normed = []
    grads = []
    for h in range(HEADS):
        now = out[h]
        normed.append(now * rscale_col)
        grad_pair = split(rscale_col * gh[h].astype(F32) - drift_col * now)
        mixed = within[h] * two(nt, grad_pair, vh[h])
        grads.append(
            FACTOR * two(nn, split(mixed), kh[h])
            + ent[h] * three(nt, grad_pair, (state_hi[h], state_lo[h]))
        )
        dkl[h] = FACTOR * two(nn, split(jnp.transpose(mixed)), qh[h])
        dvl[h] = three(nn, split(jnp.transpose(score[h])), grad_pair)
    put_heads(att_ref, normed)
    put_heads(dq_ref, grads)

    pending += row_scan(1 + 1, False, upb_in, partb, zoutb, zinb, backb)
    pending += across(3, backb, backb_in)
    arrive(3, backb_in)

    grad_keys = []
    grad_values = []
    for h in range(HEADS):
        pair = split(state_of(backb_in, h))
        grad_keys.append(dkl[h] + leave[h] * two_right(nt, vh[h], pair))
        grad_values.append(dvl[h] + leave[h] * two_right(nn, kh[h], pair))
    put_heads(dk_ref, grad_keys)
    put_heads(dv_ref, grad_values)

    for copy in pending:
        copy.wait_send()


def local(queries, key_vectors, value_vectors, out_grad, log_decay, doc_ids):
    vmem = pl.BlockSpec(memory_space=pltpu.VMEM)
    square_bf = pltpu.VMEM((HEADS, TOK, TOK), BF16)
    square_f = pltpu.VMEM((HEADS, TOK, TOK), F32)
    slices = pltpu.VMEM((ROW, HALF, TOK), F32)
    scan = [slices] * 5 + [pltpu.VMEM((2, HALF, TOK), F32), pltpu.VMEM((3, HALF, TOK), F32)]
    dma = pltpu.SemaphoreType.DMA
    result = jax.ShapeDtypeStruct((TOK, WIDTH), BF16)
    return pl.pallas_call(
        kernel,
        out_shape=[result] * 4,
        in_specs=[vmem] * 6,
        out_specs=[vmem] * 4,
        scratch_shapes=[square_bf] * 4
        + [square_f] * 6
        + [square_bf] * 4
        + [square_f] * 2
        + scan * 2
        + [pltpu.VMEM((8, TOK), F32), pltpu.VMEM((HEAD_DEVS, 8, TOK), F32)]
        + [dma((4, ROW)), dma((4, ROW)), dma((4, 3)), dma((4, 3)), dma((8,)), dma((8,))],
        compiler_params=pltpu.CompilerParams(
            collective_id=0, has_side_effects=True, vmem_limit_bytes=32 << 20
        ),
    )(
        queries, key_vectors, value_vectors, out_grad, log_decay,
        doc_ids.reshape(ROW * ROWS, TOK),
    )


def solution(mesh):
    return jax.shard_map(
        local,
        mesh=mesh,
        in_specs=(
            P("ctx", "head"), P("ctx", "head"), P("ctx", "head"), P("ctx", "head"),
            P("head", "ctx"), P(),
        ),
        out_specs=(P("ctx", "head"),) * 4,
        check_vma=False,
    )
```

time: 628 us -> 75.9 us (0.12)
  the two profiles are of different devices: /device:TPU:6 before, /device:TPU:2 now
where the time goes in v1:
time: 75.9 us; the launch traced here: 75.5 us
  Pallas kernels  67.3 us (89%)
  local copies, waits for them, and re-layouts  7.6 us (10%)
    pallas_call x1, Pallas kernels, local(): pl.pallas_call(kernel, out_shape=[result] * 4, in_specs=[vmem] * 6, out_s...  67.3 us
    unnamed x16, local copies, waits for them, and re-layouts  7.6 us

profile of v1, /device:TPU:2, one launch (start us, length us, event | category | flops | bytes accessed | tf_op | source)
XLA Modules:
  0.0 75.5 jit_solution(18059226966442987023)
XLA Ops:
  0.6 0.0 copy-start
  0.6 0.9 %copy-done = bf16[128,384]{1,0:T(8,128)(2,1)S(1)} copy-done((bf16[128,384]{1,0:T(8,128)(2,1)S(1)}, bf16[128,384]{1,0:T(8,128)(2,1)}, u32[]{:S(2)}) %copy-start) | copy-done | bytes 98328
  1.5 0.0 copy-start.1
  1.5 0.9 %copy-done.1 = bf16[128,384]{1,0:T(8,128)(2,1)S(1)} copy-done((bf16[128,384]{1,0:T(8,128)(2,1)S(1)}, bf16[128,384]{1,0:T(8,128)(2,1)}, u32[]{:S(2)}) %copy-start.1) | copy-done | bytes 98328
  2.4 0.0 copy-start.2
  2.4 0.9 %copy-done.2 = bf16[128,384]{1,0:T(8,128)(2,1)S(1)} copy-done((bf16[128,384]{1,0:T(8,128)(2,1)S(1)}, bf16[128,384]{1,0:T(8,128)(2,1)}, u32[]{:S(2)}) %copy-start.2) | copy-done | bytes 98328
  3.3 0.0 copy-start.3
  3.3 0.9 %copy-done.3 = bf16[128,384]{1,0:T(8,128)(2,1)S(1)} copy-done((bf16[128,384]{1,0:T(8,128)(2,1)S(1)}, bf16[128,384]{1,0:T(8,128)(2,1)}, u32[]{:S(2)}) %copy-start.3) | copy-done | bytes 98328
  4.2 0.0 copy-start.4
  4.2 0.8 %copy-done.4 = s32[12288]{0:T(1024)S(1)} copy-done((s32[12288]{0:T(1024)S(1)}, s32[12288]{0:T(1024)}, u32[]{:S(2)}) %copy-start.4) | copy-done | bytes 49176
  5.0 0.0 copy-start.5
  5.0 0.7 copy-done.5
  5.7 67.3 %shard_map.93 = (bf16[128,384]{1,0:T(8,128)(2,1)S(1)}, bf16[128,384]{1,0:T(8,128)(2,1)S(1)}, bf16[128,384]{1,0:T(8,128)(2,1)S(1)}, bf16[128,384]{1,0:T(8,128)(2,1)S(1)}) custom-call(bf16[128,384]{1,0:T(8,128)(2,1)S(1)} %copy-done, bf16[128,384]{1,0:T(8,128)(2,1)S(1)} %copy-done.1, bf16[128,384]{1,0:T(8,128)(2,1)S(1)} %copy-done.2, ...), custom_call_target="tpu_custom_call" | custom-call | tf_op jit(solution)/shard_map/pallas_call | solution.py:323
  73.0 0.6 copy.14
  73.6 0.6 copy.15
  74.3 0.6 copy.16
  74.9 0.6 copy.17
Async XLA Ops:
  0.6 0.9 %copy-start = (bf16[128,384]{1,0:T(8,128)(2,1)S(1)}, bf16[128,384]{1,0:T(8,128)(2,1)}, u32[]{:S(2)}) copy-start(bf16[128,384]{1,0:T(8,128)(2,1)} %q_ref.1) | copy-start | bytes 294916
  1.5 0.9 %copy-start.1 = (bf16[128,384]{1,0:T(8,128)(2,1)S(1)}, bf16[128,384]{1,0:T(8,128)(2,1)}, u32[]{:S(2)}) copy-start(bf16[128,384]{1,0:T(8,128)(2,1)} %k_ref.1) | copy-start | bytes 294916
  2.4 0.9 %copy-start.2 = (bf16[128,384]{1,0:T(8,128)(2,1)S(1)}, bf16[128,384]{1,0:T(8,128)(2,1)}, u32[]{:S(2)}) copy-start(bf16[128,384]{1,0:T(8,128)(2,1)} %v_ref.1) | copy-start | bytes 294916
  3.3 0.9 %copy-start.3 = (bf16[128,384]{1,0:T(8,128)(2,1)S(1)}, bf16[128,384]{1,0:T(8,128)(2,1)}, u32[]{:S(2)}) copy-start(bf16[128,384]{1,0:T(8,128)(2,1)} %g_ref.1) | copy-start | bytes 294916
  4.2 0.8 %copy-start.4 = (s32[12288]{0:T(1024)S(1)}, s32[12288]{0:T(1024)}, u32[]{:S(2)}) copy-start(s32[12288]{0:T(1024)} %param.11) | copy-start | bytes 147460
  5.0 0.7 copy-start.5

commit v2 on v1

--- a/solution.py
+++ b/solution.py
@@ -13,7 +13,8 @@
 ROW = 8
 ROWS = 12
 HEAD_DEVS = 8
-HALF = DH // 2
+PART = 40
+ORDER = (4, 3, 5, 2, 6, 1, 7)
 EPS = 1e-05
 FACTOR = DH ** (-0.5)
 F32 = jnp.float32
@@ -47,8 +48,10 @@
 
 
 def kernel(
-    q_ref, k_ref, v_ref, g_ref, ld_ref, doc_ref,
-    att_ref, dq_ref, dk_ref, dv_ref,
+    q_hbm, k_hbm, v_hbm, g_hbm, ld_hbm, doc_hbm,
+    att_hbm, dq_hbm, dk_hbm, dv_hbm,
+    att_ref, dq_ref, dk_ref, dv_ref, out_sem,
+    q_ref, k_ref, v_ref, g_ref, ld_ref, doc_ref, in_sem,
     qh, kh, vh, gh, qt, within, score, ent, leave, out, state_hi, state_lo,
     out_hi, out_lo, dkl, dvl,
     up, up_in, part, back, back_in, zout, zin,
@@ -76,10 +79,25 @@
             barrier, inc=1, device_id=(ctx, lax.rem(head + step, HEAD_DEVS)), device_id_type=MESH
         )
 
+    loads = [
+        pltpu.make_async_copy(src, dst, in_sem.at[n])
+        for n, (src, dst) in enumerate((
+            (ld_hbm, ld_ref), (doc_hbm, doc_ref), (k_hbm, k_ref),
+            (v_hbm, v_ref), (q_hbm, q_ref), (g_hbm, g_ref),
+        ))
+    ]
+    for load in loads:
+        load.start()
+
     lane = lax.broadcasted_iota(jnp.int32, (TOK, TOK), 1)
     sub = lax.broadcasted_iota(jnp.int32, (TOK, TOK), 0)
     real = lane < DH
-    real_half = lax.broadcasted_iota(jnp.int32, (HALF, TOK), 1) < DH
+    odd = lax.rem(y, 2)
+    part_sub = lax.broadcasted_iota(jnp.int32, (PART, TOK), 0)
+    data = (part_sub < 32) | (part_sub // 4 == 8 + odd)
+    wide = lax.broadcasted_iota(jnp.int32, (72, TOK), 1) < DH
+    third = lax.broadcasted_iota(jnp.int32, (24, TOK), 1)
+    low = lax.broadcasted_iota(jnp.int32, (8, TOK), 0) < 4
 
     def heads_of(ref):
         tiles = [ref[:, TOK * t : TOK * t + TOK].astype(F32) for t in range(3)]
@@ -101,6 +119,8 @@
     def spread(row):
         return jnp.transpose(jnp.broadcast_to(row, (TOK, TOK)))
 
+    loads[0].wait()
+    loads[1].wait()
     upper = (sub <= lane).astype(F32)
     sums = lax.dot_general(
         ld_ref[...], upper, (((1,), (0,)), ((), ())),
@@ -118,6 +138,33 @@
     enter_col = (doc_col == before).astype(F32)
     leave_col = (doc_col == last).astype(F32)
 
+    def pack(state, decay, slot, dest):
+        tail = state[72:96]
+        rest = jnp.concatenate(
+            [pltpu.roll(tail, 96, 1), pltpu.roll(tail, 64, 1), pltpu.roll(tail, 32, 1)], axis=0
+        )
+        full = jnp.where(wide, state[0:72], rest)
+        dest[slot, 0:32] = full[0:32]
+        dest[slot, 32:40] = jnp.where(low, full[32:40], decay)
+        dest[slot + 1, 0:32] = full[40:72]
+        dest[slot + 1, 32:40] = jnp.where(low, decay, full[32:40])
+
+    def unpack(arrived, h):
+        one, other = arrived[2 * h], arrived[2 * h + 1]
+        full = jnp.concatenate(
+            [one[0:32], jnp.where(low, one[32:40], other[32:40]), other[0:32]], axis=0
+        )
+        tail = jnp.where(
+            third < 32, pltpu.roll(full[0:24], 32, 1),
+            jnp.where(third < 64, pltpu.roll(full[24:48], 64, 1), pltpu.roll(full[48:72], 96, 1)),
+        )
+        tail = jnp.where(third < DH, tail, 0.0)
+        return jnp.concatenate(
+            [jnp.where(wide, full, 0.0), tail, jnp.zeros((TOK - DH, TOK), F32)], axis=0
+        )
+
+    loads[2].wait()
+    loads[3].wait()
     k_heads = heads_of(k_ref)
     v_heads = heads_of(v_ref)
     passing = []
@@ -130,9 +177,7 @@
         kh[h] = k_heads[h].astype(BF16)
         kt = jnp.transpose(k_heads[h]) * (jnp.exp(final - row) * leave_row)
         update = two(nn, split(kt), vb)
-        tile = jnp.where(real, update, passing[h])
-        up[2 * h] = tile[0:HALF]
-        up[2 * h + 1] = tile[HALF:DH]
+        pack(update, passing[h], 2 * h, up)
 
     pl.semaphore_wait(barrier, (ROW - 1) + 4 + (HEAD_DEVS - 1))
 
@@ -144,7 +189,7 @@
 
     def across(phase, src, dst):
         copies = []
-        for step in range(1, ROW):
+        for step in ORDER:
             other = lax.rem(y + step, ROW)
             copy = remote(
                 src.at[other], dst.at[y], a_send.at[phase, step], a_recv.at[phase, y],
@@ -164,15 +209,16 @@
             ).wait_recv()
 
     def factor_of(tile):
-        return jnp.broadcast_to(tile[:, DH : DH + 1], tile.shape)
+        row = jnp.where(odd == 1, tile[32:33], tile[36:37])
+        return jnp.broadcast_to(row, (PART, TOK))
 
     def join(near, far):
-        return jnp.where(real_half, near, 0.0) + factor_of(near) * far
-
-    def row_scan(base, forward, arrived, prefix, zo, zi, result):
+        return jnp.where(data, near, 0.0) + factor_of(near) * far
+
+    def row_scan(base, forward, arrived, prefix, zo, zi, result, returned):
         arrive(base, arrived)
         order = range(ROW) if forward else range(ROW - 1, -1, -1)
-        running = jnp.where(real_half, 0.0, 1.0)
+        running = jnp.where(data, 0.0, 1.0)
         for place in order:
             prefix[place] = running
             running = join(arrived[place], running)
@@ -196,19 +242,25 @@
         sends.append(copy)
         copy.wait_recv()
         entry = pair + factor_of(pair) * zi[2]
-        for place in range(ROW):
-            tile = prefix[place]
-            result[place] = tile + factor_of(tile) * entry
+        for step in ORDER:
+            other = lax.rem(y + step, ROW)
+            tile = prefix[other]
+            result[pl.ds(other, 1)] = (tile + factor_of(tile) * entry)[None]
+            copy = remote(
+                result.at[other], returned.at[y], a_send.at[base + 1, step],
+                a_recv.at[base + 1, y], (z * ROW + other, head),
+            )
+            copy.start()
+            sends.append(copy)
+        tile = prefix[y]
+        returned[pl.ds(y, 1)] = (tile + factor_of(tile) * entry)[None]
+        arrive(base + 1, returned)
         return sends
 
-    def state_of(arrived, h):
-        tile = jnp.concatenate(
-            [arrived[2 * h], arrived[2 * h + 1], jnp.zeros((TOK - DH, TOK), F32)], axis=0
-        )
-        return jnp.where(real, tile, 0.0)
-
     pending = across(0, up, up_in)
 
+    loads[4].wait()
+    loads[5].wait()
     q_heads = heads_of(q_ref)
     g_heads = heads_of(g_ref)
     for h in range(HEADS):
@@ -227,14 +279,12 @@
         score[h] = scores
         out[h] = two(nn, split(scores), vh[h])
 
-    pending += row_scan(0, True, up_in, part, zout, zin, back)
-    pending += across(1, back, back_in)
-    arrive(1, back_in)
+    pending += row_scan(0, True, up_in, part, zout, zin, back, back_in)
 
     squares = jnp.zeros((TOK, TOK), F32)
     dots = jnp.zeros((TOK, TOK), F32)
     for h in range(HEADS):
-        pair = split(state_of(back_in, h))
+        pair = split(unpack(back_in, h))
         state_hi[h] = pair[0]
         state_lo[h] = pair[1]
         now = out[h] + ent[h] * two_right(nn, qh[h], pair)
@@ -271,9 +321,7 @@
         near = split(qt[h] * rscale)
         far = split(qt[h] * drift)
         pulled = two(nn, near, gh[h]) - three(nn, far, (out_hi[h], out_lo[h]))
-        tile = jnp.where(real, pulled, passing[h])
-        upb[2 * h] = tile[0:HALF]
-        upb[2 * h + 1] = tile[HALF:DH]
+        pack(pulled, passing[h], 2 * h, upb)
 
     pending += across(2, upb, upb_in)
 
@@ -294,38 +342,58 @@
         dvl[h] = three(nn, split(jnp.transpose(score[h])), grad_pair)
     put_heads(att_ref, normed)
     put_heads(dq_ref, grads)
-
-    pending += row_scan(1 + 1, False, upb_in, partb, zoutb, zinb, backb)
-    pending += across(3, backb, backb_in)
-    arrive(3, backb_in)
-
-    grad_keys = []
-    grad_values = []
-    for h in range(HEADS):
-        pair = split(state_of(backb_in, h))
-        grad_keys.append(dkl[h] + leave[h] * two_right(nt, vh[h], pair))
-        grad_values.append(dvl[h] + leave[h] * two_right(nn, kh[h], pair))
-    put_heads(dk_ref, grad_keys)
-    put_heads(dv_ref, grad_values)
-
+    stores = [
+        pltpu.make_async_copy(src, dst, out_sem.at[n])
+        for n, (src, dst) in enumerate(
+            ((att_ref, att_hbm), (dq_ref, dq_hbm), (dk_ref, dk_hbm), (dv_ref, dv_hbm))
+        )
+    ]
+    stores[0].start()
+    stores[1].start()
+
+    pending += row_scan(2, False, upb_in, partb, zoutb, zinb, backb, backb_in)
+
+    state_pairs = [split(unpack(backb_in, h)) for h in range(HEADS)]
+    put_heads(
+        dk_ref, [dkl[h] + leave[h] * two_right(nt, vh[h], state_pairs[h]) for h in range(HEADS)]
+    )
+    stores[2].start()
+    put_heads(
+        dv_ref, [dvl[h] + leave[h] * two_right(nn, kh[h], state_pairs[h]) for h in range(HEADS)]
+    )
+    stores[3].start()
     for copy in pending:
         copy.wait_send()
+    for store in stores:
+        store.wait()
+
+
+def write(*refs):
+    srcs, dsts, sem = refs[0:4], refs[4:8], refs[8]
+    copies = [pltpu.make_async_copy(a, b, sem.at[n]) for n, (a, b) in enumerate(zip(srcs, dsts))]
+    for copy in copies:
+        copy.start()
+    for copy in copies:
+        copy.wait()
 
 
 def local(queries, key_vectors, value_vectors, out_grad, log_decay, doc_ids):
-    vmem = pl.BlockSpec(memory_space=pltpu.VMEM)
     square_bf = pltpu.VMEM((HEADS, TOK, TOK), BF16)
     square_f = pltpu.VMEM((HEADS, TOK, TOK), F32)
-    slices = pltpu.VMEM((ROW, HALF, TOK), F32)
-    scan = [slices] * 5 + [pltpu.VMEM((2, HALF, TOK), F32), pltpu.VMEM((3, HALF, TOK), F32)]
+    slices = pltpu.VMEM((ROW, PART, TOK), F32)
+    scan = [slices] * 5 + [pltpu.VMEM((2, PART, TOK), F32), pltpu.VMEM((3, PART, TOK), F32)]
     dma = pltpu.SemaphoreType.DMA
     result = jax.ShapeDtypeStruct((TOK, WIDTH), BF16)
-    return pl.pallas_call(
+    hbm = pl.BlockSpec(memory_space=pltpu.HBM)
+    results = pl.pallas_call(
         kernel,
         out_shape=[result] * 4,
-        in_specs=[vmem] * 6,
-        out_specs=[vmem] * 4,
-        scratch_shapes=[square_bf] * 4
+        in_specs=[hbm] * 6,
+        out_specs=[hbm] * 4,
+        scratch_shapes=[pltpu.VMEM((TOK, WIDTH), BF16)] * 4 + [dma((4,))]
+        + [pltpu.VMEM((TOK, WIDTH), BF16)] * 4
+        + [pltpu.VMEM((HEADS, TOK), F32), pltpu.VMEM((ROW * ROWS, TOK), jnp.int32), dma((6,))]
+        + [square_bf] * 4
         + [square_f] * 6
         + [square_bf] * 4
         + [square_f] * 2
@@ -333,12 +401,19 @@
         + [pltpu.VMEM((8, TOK), F32), pltpu.VMEM((HEAD_DEVS, 8, TOK), F32)]
         + [dma((4, ROW)), dma((4, ROW)), dma((4, 3)), dma((4, 3)), dma((8,)), dma((8,))],
         compiler_params=pltpu.CompilerParams(
-            collective_id=0, has_side_effects=True, vmem_limit_bytes=32 << 20
+            collective_id=0, has_side_effects=True, vmem_limit_bytes=60 << 20
         ),
     )(
         queries, key_vectors, value_vectors, out_grad, log_decay,
         doc_ids.reshape(ROW * ROWS, TOK),
     )
+    return pl.pallas_call(
+        write,
+        out_shape=[result] * 4,
+        in_specs=[pl.BlockSpec(memory_space=pltpu.VMEM)] * 4,
+        out_specs=[hbm] * 4,
+        scratch_shapes=[dma((4,))],
+    )(*results)
 
 
 def solution(mesh):

time: 75.9 us -> 64.3 us (0.85)
  the two profiles are of different devices: /device:TPU:2 before, /device:TPU:8 now
where the time goes in v2:
time: 64.3 us; the launch traced here: 64.1 us
  Pallas kernels  63.5 us (99%)
    pallas_call x1, Pallas kernels, local(): pl.pallas_call(kernel, out_shape=[result] * 4, in_specs=[hbm] * 6, out_sp...  61.7 us
    pallas_call x1, Pallas kernels, local(): pl.pallas_call(write, out_shape=[result] * 4, in_specs=[pl.BlockSpec(memo...  1.81 us

profile of v2, /device:TPU:8, one launch (start us, length us, event | category | flops | bytes accessed | tf_op | source)
XLA Modules:
  0.0 64.1 jit_solution(9968801339167312410)
XLA Ops:
  0.6 61.7 %shard_map.93 = (bf16[128,384]{1,0:T(8,128)(2,1)}, bf16[128,384]{1,0:T(8,128)(2,1)}, bf16[128,384]{1,0:T(8,128)(2,1)}, bf16[128,384]{1,0:T(8,128)(2,1)}) custom-call(bf16[128,384]{1,0:T(8,128)(2,1)} %q_hbm.1, bf16[128,384]{1,0:T(8,128)(2,1)} %k_hbm.1, bf16[128,384]{1,0:T(8,128)(2,1)} %v_hbm.1, bf16[128,384]{1,0:T(8,128)(2,1)} %g_hbm.1, f32[4,128]{1,0:T(4,128)} %ld_hbm.1, ...), custom_call_target="tpu_custom_call" | custom-call | tf_op jit(solution)/shard_map/pallas_call | solution.py:388
  62.3 1.8 %shard_map.94 = (bf16[128,384]{1,0:T(8,128)(2,1)}, bf16[128,384]{1,0:T(8,128)(2,1)}, bf16[128,384]{1,0:T(8,128)(2,1)}, bf16[128,384]{1,0:T(8,128)(2,1)}) custom-call(bf16[128,384]{1,0:T(8,128)(2,1)} %get-tuple-element.8.refs_0_, bf16[128,384]{1,0:T(8,128)(2,1)} %get-tuple-element.9.refs_1_, bf16[128,384]{1,0:T(8,128)(2,1)} %get-tuple-element.10.refs_2_, ...), custom_call_target="tpu_custom_call" | custom-call | tf_op jit(solution)/shard_map/pallas_call | solution.py:410

commit v3 on v2

--- a/solution.py
+++ b/solution.py
@@ -73,7 +73,11 @@
             barrier, inc=1, device_id=(z * ROW + lax.rem(y + step, ROW), head), device_id_type=MESH
         )
     for step in (-2, -1, 1, 2):
-        pl.semaphore_signal(barrier, inc=1, device_id=(at_row(step), head), device_id_type=MESH)
+
+        @pl.when((z + step >= 0) & (z + step < ROWS))
+        def _(step=step):
+            pl.semaphore_signal(barrier, inc=1, device_id=(at_row(step), head), device_id_type=MESH)
+
     for step in range(1, HEAD_DEVS):
         pl.semaphore_signal(
             barrier, inc=1, device_id=(ctx, lax.rem(head + step, HEAD_DEVS)), device_id_type=MESH
@@ -179,7 +183,8 @@
         update = two(nn, split(kt), vb)
         pack(update, passing[h], 2 * h, up)
 
-    pl.semaphore_wait(barrier, (ROW - 1) + 4 + (HEAD_DEVS - 1))
+    rows_near = jnp.minimum(z, 2) + jnp.minimum(ROWS - 1 - z, 2)
+    pl.semaphore_wait(barrier, (ROW - 1) + (HEAD_DEVS - 1) + rows_near)
 
     def remote(src, dst, send_sem, recv_sem, target):
         return pltpu.make_async_remote_copy(
@@ -196,7 +201,7 @@
                 (z * ROW + other, head),
             )
             copy.start()
-            copies.append(copy)
+            copies.append((None, copy))
         dst[pl.ds(y, 1)] = src[pl.ds(y, 1)]
         return copies
 
@@ -224,23 +229,45 @@
             running = join(arrived[place], running)
         zo[0] = running
         sign = 1 if forward else -1
+        place_z = z if forward else ROWS - 1 - z
+        for n in range(3):
+
+            @pl.when(place_z <= n)
+            def _(n=n):
+                zi[n] = jnp.zeros((PART, TOK), F32)
+
+        def hop(n):
+            distance = 1 if n == 0 else 2
+            return remote(
+                zo.at[n // 2], zi.at[n], z_send.at[base, n], z_recv.at[base, n],
+                (at_row(sign * distance), head),
+            )
+
+        sending = (place_z < ROWS - 1, place_z < ROWS - 2, (place_z > 0) & (place_z < ROWS - 2))
         sends = []
-        for n, (slot, step) in enumerate(((0, sign), (0, 2 * sign))):
-            copy = remote(
-                zo.at[slot], zi.at[n], z_send.at[base, n], z_recv.at[base, n], (at_row(step), head)
-            )
-            copy.start()
-            sends.append(copy)
-        sends[0].wait_recv()
-        sends[1].wait_recv()
+
+        def send_hop(n):
+            copy = hop(n)
+
+            @pl.when(sending[n])
+            def _():
+                copy.start()
+
+            sends.append((sending[n], copy))
+
+        def get_hop(n):
+            @pl.when(place_z > n)
+            def _():
+                hop(n).wait_recv()
+
+        send_hop(1)
+        send_hop(0)
+        get_hop(0)
+        get_hop(1)
         pair = join(zi[0], zi[1])
         zo[1] = pair
-        copy = remote(
-            zo.at[1], zi.at[2], z_send.at[base, 2], z_recv.at[base, 2], (at_row(2 * sign), head)
-        )
-        copy.start()
-        sends.append(copy)
-        copy.wait_recv()
+        send_hop(2)
+        get_hop(2)
         entry = pair + factor_of(pair) * zi[2]
         for step in ORDER:
             other = lax.rem(y + step, ROW)
@@ -251,7 +278,7 @@
                 a_recv.at[base + 1, y], (z * ROW + other, head),
             )
             copy.start()
-            sends.append(copy)
+            sends.append((None, copy))
         tile = prefix[y]
         returned[pl.ds(y, 1)] = (tile + factor_of(tile) * entry)[None]
         arrive(base + 1, returned)
@@ -300,7 +327,7 @@
         other = lax.rem(head + step, HEAD_DEVS)
         copy = remote(hsend, hrecv.at[head], h_send.at[step], h_recv.at[head], (ctx, other))
         copy.start()
-        pending.append(copy)
+        pending.append((None, copy))
     hrecv[pl.ds(head, 1)] = tile[None]
     for h in range(HEADS):
         pair = split(out[h])
@@ -362,8 +389,11 @@
         dv_ref, [dvl[h] + leave[h] * two_right(nn, kh[h], state_pairs[h]) for h in range(HEADS)]
     )
     stores[3].start()
-    for copy in pending:
-        copy.wait_send()
+    for condition, copy in pending:
+        if condition is None:
+            copy.wait_send()
+        else:
+            pl.when(condition)(copy.wait_send)
     for store in stores:
         store.wait()
 

time: 64.3 us -> 57.1 us (0.89)
  the two profiles are of different devices: /device:TPU:8 before, /device:TPU:6 now
where the time goes in v3:
time: 57.1 us; the launch traced here: 56.6 us
  Pallas kernels  56 us (98%)
  between operations  0.64 us (1%)
    pallas_call x1, Pallas kernels, local(): pl.pallas_call(kernel, out_shape=[result] * 4, in_specs=[hbm] * 6, out_sp...  54.2 us
    pallas_call x1, Pallas kernels, local(): pl.pallas_call(write, out_shape=[result] * 4, in_specs=[pl.BlockSpec(memo...  1.81 us

profile of v3, /device:TPU:6, one launch (start us, length us, event | category | flops | bytes accessed | tf_op | source)
XLA Modules:
  0.0 56.6 jit_solution(1749235501380528034)
XLA Ops:
  0.6 54.2 %shard_map.93 = (bf16[128,384]{1,0:T(8,128)(2,1)}, bf16[128,384]{1,0:T(8,128)(2,1)}, bf16[128,384]{1,0:T(8,128)(2,1)}, bf16[128,384]{1,0:T(8,128)(2,1)}) custom-call(bf16[128,384]{1,0:T(8,128)(2,1)} %q_hbm.1, bf16[128,384]{1,0:T(8,128)(2,1)} %k_hbm.1, bf16[128,384]{1,0:T(8,128)(2,1)} %v_hbm.1, bf16[128,384]{1,0:T(8,128)(2,1)} %g_hbm.1, f32[4,128]{1,0:T(4,128)} %ld_hbm.1, ...), custom_call_target="tpu_custom_call" | custom-call | tf_op jit(solution)/shard_map/pallas_call | solution.py:418
  54.8 1.8 %shard_map.94 = (bf16[128,384]{1,0:T(8,128)(2,1)}, bf16[128,384]{1,0:T(8,128)(2,1)}, bf16[128,384]{1,0:T(8,128)(2,1)}, bf16[128,384]{1,0:T(8,128)(2,1)}) custom-call(bf16[128,384]{1,0:T(8,128)(2,1)} %get-tuple-element.8.refs_0_, bf16[128,384]{1,0:T(8,128)(2,1)} %get-tuple-element.9.refs_1_, bf16[128,384]{1,0:T(8,128)(2,1)} %get-tuple-element.10.refs_2_, ...), custom_call_target="tpu_custom_call" | custom-call | tf_op jit(solution)/shard_map/pallas_call | solution.py:440

commit v4 on v3

--- a/solution.py
+++ b/solution.py
@@ -14,6 +14,7 @@
 ROWS = 12
 HEAD_DEVS = 8
 PART = 40
+USED = 36
 ORDER = (4, 3, 5, 2, 6, 1, 7)
 EPS = 1e-05
 FACTOR = DH ** (-0.5)
@@ -49,8 +50,7 @@
 
 def kernel(
     q_hbm, k_hbm, v_hbm, g_hbm, ld_hbm, doc_hbm,
-    att_hbm, dq_hbm, dk_hbm, dv_hbm,
-    att_ref, dq_ref, dk_ref, dv_ref, out_sem,
+    att_ref, dq_ref, dk_ref, dv_ref,
     q_ref, k_ref, v_ref, g_ref, ld_ref, doc_ref, in_sem,
     qh, kh, vh, gh, qt, within, score, ent, leave, out, state_hi, state_lo,
     out_hi, out_lo, dkl, dvl,
@@ -96,9 +96,8 @@
     lane = lax.broadcasted_iota(jnp.int32, (TOK, TOK), 1)
     sub = lax.broadcasted_iota(jnp.int32, (TOK, TOK), 0)
     real = lane < DH
-    odd = lax.rem(y, 2)
     part_sub = lax.broadcasted_iota(jnp.int32, (PART, TOK), 0)
-    data = (part_sub < 32) | (part_sub // 4 == 8 + odd)
+    data = part_sub < USED
     wide = lax.broadcasted_iota(jnp.int32, (72, TOK), 1) < DH
     third = lax.broadcasted_iota(jnp.int32, (24, TOK), 1)
     low = lax.broadcasted_iota(jnp.int32, (8, TOK), 0) < 4
@@ -151,12 +150,12 @@
         dest[slot, 0:32] = full[0:32]
         dest[slot, 32:40] = jnp.where(low, full[32:40], decay)
         dest[slot + 1, 0:32] = full[40:72]
-        dest[slot + 1, 32:40] = jnp.where(low, decay, full[32:40])
+        dest[slot + 1, 32:40] = jnp.where(low, pltpu.roll(full[32:40], 4, 0), decay)
 
     def unpack(arrived, h):
         one, other = arrived[2 * h], arrived[2 * h + 1]
         full = jnp.concatenate(
-            [one[0:32], jnp.where(low, one[32:40], other[32:40]), other[0:32]], axis=0
+            [one[0:32], jnp.where(low, one[32:40], pltpu.roll(other[32:40], 4, 0)), other[0:32]], axis=0
         )
         tail = jnp.where(
             third < 32, pltpu.roll(full[0:24], 32, 1),
@@ -192,12 +191,13 @@
             device_id=target, device_id_type=MESH,
         )
 
-    def across(phase, src, dst):
+    def across(phase, src, dst, rows):
         copies = []
         for step in ORDER:
             other = lax.rem(y + step, ROW)
             copy = remote(
-                src.at[other], dst.at[y], a_send.at[phase, step], a_recv.at[phase, y],
+                src.at[other, pl.ds(0, rows)], dst.at[y, pl.ds(0, rows)],
+                a_send.at[phase, step], a_recv.at[phase, y],
                 (z * ROW + other, head),
             )
             copy.start()
@@ -205,28 +205,28 @@
         dst[pl.ds(y, 1)] = src[pl.ds(y, 1)]
         return copies
 
-    def arrive(phase, dst):
+    def arrive(phase, dst, rows):
         for step in range(1, ROW):
             other = lax.rem(y + step, ROW)
             remote(
-                dst.at[other], dst.at[other], a_send.at[phase, step], a_recv.at[phase, other],
+                dst.at[other, pl.ds(0, rows)], dst.at[other, pl.ds(0, rows)],
+                a_send.at[phase, step], a_recv.at[phase, other],
                 (z * ROW + other, head),
             ).wait_recv()
 
     def factor_of(tile):
-        row = jnp.where(odd == 1, tile[32:33], tile[36:37])
-        return jnp.broadcast_to(row, (PART, TOK))
-
-    def join(near, far):
-        return jnp.where(data, near, 0.0) + factor_of(near) * far
+        return jnp.broadcast_to(tile[USED : USED + 1], (PART, TOK))
+
+    def join(near, far, factor):
+        return jnp.where(data, near, 0.0) + factor * far
 
     def row_scan(base, forward, arrived, prefix, zo, zi, result, returned):
-        arrive(base, arrived)
+        arrive(base, arrived, USED + 1 if forward else USED)
         order = range(ROW) if forward else range(ROW - 1, -1, -1)
         running = jnp.where(data, 0.0, 1.0)
         for place in order:
             prefix[place] = running
-            running = join(arrived[place], running)
+            running = join(arrived[place], running, factor_of(up_in[place]))
         zo[0] = running
         sign = 1 if forward else -1
         place_z = z if forward else ROWS - 1 - z
@@ -239,7 +239,7 @@
         def hop(n):
             distance = 1 if n == 0 else 2
             return remote(
-                zo.at[n // 2], zi.at[n], z_send.at[base, n], z_recv.at[base, n],
+                zo.at[n // 2, pl.ds(0, USED + 1)], zi.at[n, pl.ds(0, USED + 1)], z_send.at[base, n], z_recv.at[base, n],
                 (at_row(sign * distance), head),
             )
 
@@ -264,7 +264,7 @@
         send_hop(0)
         get_hop(0)
         get_hop(1)
-        pair = join(zi[0], zi[1])
+        pair = join(zi[0], zi[1], factor_of(zi[0]))
         zo[1] = pair
         send_hop(2)
         get_hop(2)
@@ -274,17 +274,17 @@
             tile = prefix[other]
             result[pl.ds(other, 1)] = (tile + factor_of(tile) * entry)[None]
             copy = remote(
-                result.at[other], returned.at[y], a_send.at[base + 1, step],
-                a_recv.at[base + 1, y], (z * ROW + other, head),
+                result.at[other, pl.ds(0, USED)], returned.at[y, pl.ds(0, USED)],
+                a_send.at[base + 1, step], a_recv.at[base + 1, y], (z * ROW + other, head),
             )
             copy.start()
             sends.append((None, copy))
         tile = prefix[y]
         returned[pl.ds(y, 1)] = (tile + factor_of(tile) * entry)[None]
-        arrive(base + 1, returned)
+        arrive(base + 1, returned, USED)
         return sends
 
-    pending = across(0, up, up_in)
+    pending = across(0, up, up_in, USED + 1)
 
     loads[4].wait()
     loads[5].wait()
@@ -325,7 +325,7 @@
     hsend[...] = tile
     for step in range(1, HEAD_DEVS):
         other = lax.rem(head + step, HEAD_DEVS)
-        copy = remote(hsend, hrecv.at[head], h_send.at[step], h_recv.at[head], (ctx, other))
+        copy = remote(hsend.at[pl.ds(0, 2)], hrecv.at[head, pl.ds(0, 2)], h_send.at[step], h_recv.at[head], (ctx, other))
         copy.start()
         pending.append((None, copy))
     hrecv[pl.ds(head, 1)] = tile[None]
@@ -336,11 +336,11 @@
     for step in range(1, HEAD_DEVS):
         other = lax.rem(head + step, HEAD_DEVS)
         remote(
-            hrecv.at[other], hrecv.at[other], h_send.at[step], h_recv.at[other], (ctx, other)
+            hrecv.at[other, pl.ds(0, 2)], hrecv.at[other, pl.ds(0, 2)], h_send.at[step], h_recv.at[other], (ctx, other)
         ).wait_recv()
-    total = hrecv[0]
+    total = hrecv[0, 0:2]
     for slot in range(1, HEAD_DEVS):
-        total = total + hrecv[slot]
+        total = total + hrecv[slot, 0:2]
     rscale = lax.rsqrt(total[0:1] / FULL + EPS)
     drift = rscale * rscale * rscale * total[1:2] / FULL
 
@@ -350,7 +350,7 @@
         pulled = two(nn, near, gh[h]) - three(nn, far, (out_hi[h], out_lo[h]))
         pack(pulled, passing[h], 2 * h, upb)
 
-    pending += across(2, upb, upb_in)
+    pending += across(2, upb, upb_in, USED)
 
     rscale_col = spread(rscale)
     drift_col = spread(drift)
@@ -369,14 +369,6 @@
         dvl[h] = three(nn, split(jnp.transpose(score[h])), grad_pair)
     put_heads(att_ref, normed)
     put_heads(dq_ref, grads)
-    stores = [
-        pltpu.make_async_copy(src, dst, out_sem.at[n])
-        for n, (src, dst) in enumerate(
-            ((att_ref, att_hbm), (dq_ref, dq_hbm), (dk_ref, dk_hbm), (dv_ref, dv_hbm))
-        )
-    ]
-    stores[0].start()
-    stores[1].start()
 
     pending += row_scan(2, False, upb_in, partb, zoutb, zinb, backb, backb_in)
 
@@ -384,18 +376,14 @@
     put_heads(
         dk_ref, [dkl[h] + leave[h] * two_right(nt, vh[h], state_pairs[h]) for h in range(HEADS)]
     )
-    stores[2].start()
     put_heads(
         dv_ref, [dvl[h] + leave[h] * two_right(nn, kh[h], state_pairs[h]) for h in range(HEADS)]
     )
-    stores[3].start()
     for condition, copy in pending:
         if condition is None:
             copy.wait_send()
         else:
             pl.when(condition)(copy.wait_send)
-    for store in stores:
-        store.wait()
 
 
 def write(*refs):
@@ -414,14 +402,21 @@
     scan = [slices] * 5 + [pltpu.VMEM((2, PART, TOK), F32), pltpu.VMEM((3, PART, TOK), F32)]
     dma = pltpu.SemaphoreType.DMA
     result = jax.ShapeDtypeStruct((TOK, WIDTH), BF16)
+    vmem = pl.BlockSpec(memory_space=pltpu.VMEM)
     hbm = pl.BlockSpec(memory_space=pltpu.HBM)
+    queries, key_vectors, value_vectors, out_grad, log_decay, docs = (
+        pltpu.with_memory_space_constraint(x, pltpu.HBM)
+        for x in (
+            queries, key_vectors, value_vectors, out_grad, log_decay,
+            doc_ids.reshape(ROW * ROWS, TOK),
+        )
+    )
     results = pl.pallas_call(
         kernel,
         out_shape=[result] * 4,
         in_specs=[hbm] * 6,
-        out_specs=[hbm] * 4,
-        scratch_shapes=[pltpu.VMEM((TOK, WIDTH), BF16)] * 4 + [dma((4,))]
-        + [pltpu.VMEM((TOK, WIDTH), BF16)] * 4
+        out_specs=[vmem] * 4,
+        scratch_shapes=[pltpu.VMEM((TOK, WIDTH), BF16)] * 4
         + [pltpu.VMEM((HEADS, TOK), F32), pltpu.VMEM((ROW * ROWS, TOK), jnp.int32), dma((6,))]
         + [square_bf] * 4
         + [square_f] * 6
@@ -431,19 +426,18 @@
         + [pltpu.VMEM((8, TOK), F32), pltpu.VMEM((HEAD_DEVS, 8, TOK), F32)]
         + [dma((4, ROW)), dma((4, ROW)), dma((4, 3)), dma((4, 3)), dma((8,)), dma((8,))],
         compiler_params=pltpu.CompilerParams(
-            collective_id=0, has_side_effects=True, vmem_limit_bytes=60 << 20
+            collective_id=0, has_side_effects=True, vmem_limit_bytes=32 << 20
         ),
     )(
-        queries, key_vectors, value_vectors, out_grad, log_decay,
-        doc_ids.reshape(ROW * ROWS, TOK),
+        queries, key_vectors, value_vectors, out_grad, log_decay, docs,
     )
     return pl.pallas_call(
         write,
         out_shape=[result] * 4,
-        in_specs=[pl.BlockSpec(memory_space=pltpu.VMEM)] * 4,
+        in_specs=[vmem] * 4,
         out_specs=[hbm] * 4,
         scratch_shapes=[dma((4,))],
-    )(*results)
+    )(*(pltpu.with_memory_space_constraint(x, pltpu.VMEM) for x in results))
 
 
 def solution(mesh):

time: 57.1 us -> 54.7 us (0.958)
  Pallas kernels: 56 us -> 53.6 us
    pallas_call x1, Pallas kernels: 54.2 us -> 52.8 us  [local(): pl.pallas_call(kernel, out_shape=[result] * 4, in_specs=[hbm] * 6, out_sp...]
    pallas_call x1, Pallas kernels: 1.81 us -> 0.78 us  [local(): pl.pallas_call(write, out_shape=[result] * 4, in_specs=[vmem] * 4, out_sp...]
where the time goes in v4:
time: 54.7 us; the launch traced here: 54.2 us
  Pallas kernels  53.6 us (98%)
  between operations  0.64 us (1%)
    pallas_call x1, Pallas kernels, local(): pl.pallas_call(kernel, out_shape=[result] * 4, in_specs=[hbm] * 6, out_sp...  52.8 us

profile of v4, /device:TPU:6, one launch (start us, length us, event | category | flops | bytes accessed | tf_op | source)
XLA Modules:
  0.0 54.2 jit_solution(6238936495263514937)
XLA Ops:
  0.6 52.8 %shard_map.93 = (bf16[128,384]{1,0:T(8,128)(2,1)S(1)}, bf16[128,384]{1,0:T(8,128)(2,1)S(1)}, bf16[128,384]{1,0:T(8,128)(2,1)S(1)}, bf16[128,384]{1,0:T(8,128)(2,1)S(1)}) custom-call(bf16[128,384]{1,0:T(8,128)(2,1)} %q_hbm.1, bf16[128,384]{1,0:T(8,128)(2,1)} %k_hbm.1, bf16[128,384]{1,0:T(8,128)(2,1)} %v_hbm.1, bf16[128,384]{1,0:T(8,128)(2,1)} %g_hbm.1, ...), custom_call_target="tpu_custom_call" | custom-call | tf_op jit(solution)/shard_map/pallas_call | solution.py:414
  53.5 0.8 %shard_map.94 = (bf16[128,384]{1,0:T(8,128)(2,1)}, bf16[128,384]{1,0:T(8,128)(2,1)}, bf16[128,384]{1,0:T(8,128)(2,1)}, bf16[128,384]{1,0:T(8,128)(2,1)}) custom-call(bf16[128,384]{1,0:T(8,128)(2,1)S(1)} %get-tuple-element.8.refs_0_, bf16[128,384]{1,0:T(8,128)(2,1)S(1)} %get-tuple-element.9.refs_1_, bf16[128,384]{1,0:T(8,128)(2,1)S(1)} %get-tuple-element.10.refs_2_, ...), custom_call_target="tpu_custom_call" | custom-call | tf_op jit(solution)/shard_map/pallas_call | solution.py:434

commit v5 on v4

--- a/solution.py
+++ b/solution.py
@@ -191,28 +191,29 @@
             device_id=target, device_id_type=MESH,
         )
 
+    def wait_all(view, sem):
+        pltpu.make_async_copy(view, view, sem).wait()
+
+    def drain(copies):
+        for condition, copy in copies:
+            if condition is None:
+                copy.wait_send()
+            else:
+                pl.when(condition)(copy.wait_send)
+
     def across(phase, src, dst, rows):
-        copies = []
         for step in ORDER:
             other = lax.rem(y + step, ROW)
             copy = remote(
                 src.at[other, pl.ds(0, rows)], dst.at[y, pl.ds(0, rows)],
-                a_send.at[phase, step], a_recv.at[phase, y],
+                a_send.at[phase], a_recv.at[phase],
                 (z * ROW + other, head),
             )
             copy.start()
-            copies.append((None, copy))
         dst[pl.ds(y, 1)] = src[pl.ds(y, 1)]
-        return copies
 
     def arrive(phase, dst, rows):
-        for step in range(1, ROW):
-            other = lax.rem(y + step, ROW)
-            remote(
-                dst.at[other, pl.ds(0, rows)], dst.at[other, pl.ds(0, rows)],
-                a_send.at[phase, step], a_recv.at[phase, other],
-                (z * ROW + other, head),
-            ).wait_recv()
+        wait_all(dst.at[pl.ds(0, ROW - 1), pl.ds(0, rows)], a_recv.at[phase])
 
     def factor_of(tile):
         return jnp.broadcast_to(tile[USED : USED + 1], (PART, TOK))
@@ -275,16 +276,16 @@
             result[pl.ds(other, 1)] = (tile + factor_of(tile) * entry)[None]
             copy = remote(
                 result.at[other, pl.ds(0, USED)], returned.at[y, pl.ds(0, USED)],
-                a_send.at[base + 1, step], a_recv.at[base + 1, y], (z * ROW + other, head),
+                a_send.at[base + 1], a_recv.at[base + 1], (z * ROW + other, head),
             )
             copy.start()
-            sends.append((None, copy))
         tile = prefix[y]
         returned[pl.ds(y, 1)] = (tile + factor_of(tile) * entry)[None]
+        drain(sends)
+        wait_all(result.at[pl.ds(0, ROW - 1), pl.ds(0, USED)], a_send.at[base + 1])
         arrive(base + 1, returned, USED)
-        return sends
-
-    pending = across(0, up, up_in, USED + 1)
+
+    across(0, up, up_in, USED + 1)
 
     loads[4].wait()
     loads[5].wait()
@@ -306,7 +307,8 @@
         score[h] = scores
         out[h] = two(nn, split(scores), vh[h])
 
-    pending += row_scan(0, True, up_in, part, zout, zin, back, back_in)
+    wait_all(up.at[pl.ds(0, ROW - 1), pl.ds(0, USED + 1)], a_send.at[0])
+    row_scan(0, True, up_in, part, zout, zin, back, back_in)
 
     squares = jnp.zeros((TOK, TOK), F32)
     dots = jnp.zeros((TOK, TOK), F32)
@@ -325,19 +327,15 @@
     hsend[...] = tile
     for step in range(1, HEAD_DEVS):
         other = lax.rem(head + step, HEAD_DEVS)
-        copy = remote(hsend.at[pl.ds(0, 2)], hrecv.at[head, pl.ds(0, 2)], h_send.at[step], h_recv.at[head], (ctx, other))
+        copy = remote(hsend.at[pl.ds(0, 2)], hrecv.at[head, pl.ds(0, 2)], h_send, h_recv, (ctx, other))
         copy.start()
-        pending.append((None, copy))
     hrecv[pl.ds(head, 1)] = tile[None]
     for h in range(HEADS):
         pair = split(out[h])
         out_hi[h] = pair[0]
         out_lo[h] = pair[1]
-    for step in range(1, HEAD_DEVS):
-        other = lax.rem(head + step, HEAD_DEVS)
-        remote(
-            hrecv.at[other, pl.ds(0, 2)], hrecv.at[other, pl.ds(0, 2)], h_send.at[step], h_recv.at[other], (ctx, other)
-        ).wait_recv()
+    wait_all(hrecv.at[pl.ds(0, HEAD_DEVS - 1), pl.ds(0, 2)], h_send)
+    wait_all(hrecv.at[pl.ds(0, HEAD_DEVS - 1), pl.ds(0, 2)], h_recv)
     total = hrecv[0, 0:2]
     for slot in range(1, HEAD_DEVS):
         total = total + hrecv[slot, 0:2]
@@ -350,7 +348,7 @@
         pulled = two(nn, near, gh[h]) - three(nn, far, (out_hi[h], out_lo[h]))
         pack(pulled, passing[h], 2 * h, upb)
 
-    pending += across(2, upb, upb_in, USED)
+    across(2, upb, upb_in, USED)
 
     rscale_col = spread(rscale)
     drift_col = spread(drift)
@@ -370,7 +368,8 @@
     put_heads(att_ref, normed)
     put_heads(dq_ref, grads)
 
-    pending += row_scan(2, False, upb_in, partb, zoutb, zinb, backb, backb_in)
+    wait_all(upb.at[pl.ds(0, ROW - 1), pl.ds(0, USED)], a_send.at[2])
+    row_scan(2, False, upb_in, partb, zoutb, zinb, backb, backb_in)
 
     state_pairs = [split(unpack(backb_in, h)) for h in range(HEADS)]
     put_heads(
@@ -379,11 +378,6 @@
     put_heads(
         dv_ref, [dvl[h] + leave[h] * two_right(nn, kh[h], state_pairs[h]) for h in range(HEADS)]
     )
-    for condition, copy in pending:
-        if condition is None:
-            copy.wait_send()
-        else:
-            pl.when(condition)(copy.wait_send)
 
 
 def write(*refs):
@@ -424,7 +418,7 @@
         + [square_f] * 2
         + scan * 2
         + [pltpu.VMEM((8, TOK), F32), pltpu.VMEM((HEAD_DEVS, 8, TOK), F32)]
-        + [dma((4, ROW)), dma((4, ROW)), dma((4, 3)), dma((4, 3)), dma((8,)), dma((8,))],
+        + [dma((4,)), dma((4,)), dma((4, 3)), dma((4, 3)), dma, dma],
         compiler_params=pltpu.CompilerParams(
             collective_id=0, has_side_effects=True, vmem_limit_bytes=32 << 20
         ),

time: 54.7 us -> 53.9 us (0.985)
  Pallas kernels: 53.6 us -> 52.9 us
    pallas_call x1, Pallas kernels: 52.8 us -> 52.2 us  [local(): pl.pallas_call(kernel, out_shape=[result] * 4, in_specs=[hbm] * 6, out_sp...]
where the time goes in v5:
time: 53.9 us; the launch traced here: 53.6 us
  Pallas kernels  52.9 us (98%)
  between operations  0.64 us (1%)
    pallas_call x1, Pallas kernels, local(): pl.pallas_call(kernel, out_shape=[result] * 4, in_specs=[hbm] * 6, out_sp...  52.2 us

profile of v5, /device:TPU:6, one launch (start us, length us, event | category | flops | bytes accessed | tf_op | source)
XLA Modules:
  0.0 53.6 jit_solution(9252609493258489625)
XLA Ops:
  0.6 52.2 %shard_map.93 = (bf16[128,384]{1,0:T(8,128)(2,1)S(1)}, bf16[128,384]{1,0:T(8,128)(2,1)S(1)}, bf16[128,384]{1,0:T(8,128)(2,1)S(1)}, bf16[128,384]{1,0:T(8,128)(2,1)S(1)}) custom-call(bf16[128,384]{1,0:T(8,128)(2,1)} %q_hbm.1, bf16[128,384]{1,0:T(8,128)(2,1)} %k_hbm.1, bf16[128,384]{1,0:T(8,128)(2,1)} %v_hbm.1, bf16[128,384]{1,0:T(8,128)(2,1)} %g_hbm.1, ...), custom_call_target="tpu_custom_call" | custom-call | tf_op jit(solution)/shard_map/pallas_call | solution.py:408
  52.8 0.8 %shard_map.94 = (bf16[128,384]{1,0:T(8,128)(2,1)}, bf16[128,384]{1,0:T(8,128)(2,1)}, bf16[128,384]{1,0:T(8,128)(2,1)}, bf16[128,384]{1,0:T(8,128)(2,1)}) custom-call(bf16[128,384]{1,0:T(8,128)(2,1)S(1)} %get-tuple-element.8.refs_0_, bf16[128,384]{1,0:T(8,128)(2,1)S(1)} %get-tuple-element.9.refs_1_, bf16[128,384]{1,0:T(8,128)(2,1)S(1)} %get-tuple-element.10.refs_2_, ...), custom_call_target="tpu_custom_call" | custom-call | tf_op jit(solution)/shard_map/pallas_call | solution.py:428

commit v6 on v5

--- a/solution.py
+++ b/solution.py
@@ -15,6 +15,7 @@
 HEAD_DEVS = 8
 PART = 40
 USED = 36
+CUT = 24
 ORDER = (4, 3, 5, 2, 6, 1, 7)
 EPS = 1e-05
 FACTOR = DH ** (-0.5)
@@ -96,8 +97,7 @@
     lane = lax.broadcasted_iota(jnp.int32, (TOK, TOK), 1)
     sub = lax.broadcasted_iota(jnp.int32, (TOK, TOK), 0)
     real = lane < DH
-    part_sub = lax.broadcasted_iota(jnp.int32, (PART, TOK), 0)
-    data = part_sub < USED
+    data = lax.broadcasted_iota(jnp.int32, (PART - CUT, TOK), 0) < USED - CUT
     wide = lax.broadcasted_iota(jnp.int32, (72, TOK), 1) < DH
     third = lax.broadcasted_iota(jnp.int32, (24, TOK), 1)
     low = lax.broadcasted_iota(jnp.int32, (8, TOK), 0) < 4
@@ -201,89 +201,100 @@
             else:
                 pl.when(condition)(copy.wait_send)
 
-    def across(phase, src, dst, rows):
-        for step in ORDER:
-            other = lax.rem(y + step, ROW)
-            copy = remote(
-                src.at[other, pl.ds(0, rows)], dst.at[y, pl.ds(0, rows)],
-                a_send.at[phase], a_recv.at[phase],
-                (z * ROW + other, head),
-            )
-            copy.start()
+    def pieces(last):
+        return (pl.ds(CUT, last - CUT), pl.ds(0, CUT))
+
+    def across(phase, src, dst, last):
+        for n, rows in enumerate(pieces(last)):
+            for step in ORDER:
+                other = lax.rem(y + step, ROW)
+                remote(
+                    src.at[other, rows], dst.at[y, rows], a_send.at[phase], a_recv.at[phase, n],
+                    (z * ROW + other, head),
+                ).start()
         dst[pl.ds(y, 1)] = src[pl.ds(y, 1)]
 
-    def arrive(phase, dst, rows):
-        wait_all(dst.at[pl.ds(0, ROW - 1), pl.ds(0, rows)], a_recv.at[phase])
-
-    def factor_of(tile):
-        return jnp.broadcast_to(tile[USED : USED + 1], (PART, TOK))
-
-    def join(near, far, factor):
-        return jnp.where(data, near, 0.0) + factor * far
+    def factor_of(ref, place, rows):
+        return jnp.broadcast_to(ref[place, USED : USED + 1], (rows, TOK))
 
     def row_scan(base, forward, arrived, prefix, zo, zi, result, returned):
-        arrive(base, arrived, USED + 1 if forward else USED)
         order = range(ROW) if forward else range(ROW - 1, -1, -1)
-        running = jnp.where(data, 0.0, 1.0)
-        for place in order:
-            prefix[place] = running
-            running = join(arrived[place], running, factor_of(up_in[place]))
-        zo[0] = running
         sign = 1 if forward else -1
         place_z = z if forward else ROWS - 1 - z
+        sending = (place_z < ROWS - 1, place_z < ROWS - 2, (place_z > 0) & (place_z < ROWS - 2))
+        spans = pieces(USED + 1)
+        tiles = (slice(CUT, PART), slice(0, CUT))
+        heights = (PART - CUT, CUT)
+        sends = []
+
+        def hop(n, piece):
+            distance = 1 if n == 0 else 2
+            return remote(
+                zo.at[n // 2, spans[piece]], zi.at[n, spans[piece]],
+                z_send.at[base + piece, n], z_recv.at[base + piece, n],
+                (at_row(sign * distance), head),
+            )
+
+        def send_hop(n, piece):
+            copy = hop(n, piece)
+            pl.when(sending[n])(copy.start)
+            sends.append((sending[n], copy))
+
+        def get_hop(n, piece):
+            pl.when(place_z > n)(hop(n, piece).wait_recv)
+
+        def near_part(tile, piece):
+            return jnp.where(data, tile, 0.0) if piece == 0 else tile
+
         for n in range(3):
 
             @pl.when(place_z <= n)
             def _(n=n):
                 zi[n] = jnp.zeros((PART, TOK), F32)
 
-        def hop(n):
-            distance = 1 if n == 0 else 2
-            return remote(
-                zo.at[n // 2, pl.ds(0, USED + 1)], zi.at[n, pl.ds(0, USED + 1)], z_send.at[base, n], z_recv.at[base, n],
-                (at_row(sign * distance), head),
+        for piece in range(2):
+            rows = tiles[piece]
+            count = (USED + 1 if forward else USED) - CUT if piece == 0 else CUT
+            wait_all(
+                arrived.at[pl.ds(0, ROW - 1), pl.ds(CUT if piece == 0 else 0, count)],
+                a_recv.at[base, piece],
             )
-
-        sending = (place_z < ROWS - 1, place_z < ROWS - 2, (place_z > 0) & (place_z < ROWS - 2))
-        sends = []
-
-        def send_hop(n):
-            copy = hop(n)
-
-            @pl.when(sending[n])
-            def _():
-                copy.start()
-
-            sends.append((sending[n], copy))
-
-        def get_hop(n):
-            @pl.when(place_z > n)
-            def _():
-                hop(n).wait_recv()
-
-        send_hop(1)
-        send_hop(0)
-        get_hop(0)
-        get_hop(1)
-        pair = join(zi[0], zi[1], factor_of(zi[0]))
-        zo[1] = pair
-        send_hop(2)
-        get_hop(2)
-        entry = pair + factor_of(pair) * zi[2]
-        for step in ORDER:
-            other = lax.rem(y + step, ROW)
-            tile = prefix[other]
-            result[pl.ds(other, 1)] = (tile + factor_of(tile) * entry)[None]
-            copy = remote(
-                result.at[other, pl.ds(0, USED)], returned.at[y, pl.ds(0, USED)],
-                a_send.at[base + 1], a_recv.at[base + 1], (z * ROW + other, head),
+            running = jnp.where(data, 0.0, 1.0) if piece == 0 else jnp.zeros((CUT, TOK), F32)
+            for place in order:
+                prefix[place, rows] = running
+                running = near_part(arrived[place, rows], piece) + (
+                    factor_of(up_in, place, heights[piece]) * running
+                )
+            zo[0, rows] = running
+            send_hop(1, piece)
+            send_hop(0, piece)
+        for piece in range(2):
+            rows = tiles[piece]
+            get_hop(0, piece)
+            get_hop(1, piece)
+            zo[1, rows] = near_part(zi[0, rows], piece) + (
+                factor_of(zi, 0, heights[piece]) * zi[1, rows]
             )
-            copy.start()
-        tile = prefix[y]
-        returned[pl.ds(y, 1)] = (tile + factor_of(tile) * entry)[None]
+            send_hop(2, piece)
+        returning = pieces(USED)
+        for piece in range(2):
+            rows = tiles[piece]
+            get_hop(2, piece)
+            entry = zo[1, rows] + factor_of(zo, 1, heights[piece]) * zi[2, rows]
+            for step in ORDER:
+                other = lax.rem(y + step, ROW)
+                result[other, rows] = (
+                    prefix[other, rows] + factor_of(prefix, other, heights[piece]) * entry
+                )
+                remote(
+                    result.at[other, returning[piece]], returned.at[y, returning[piece]],
+                    a_send.at[base + 1], a_recv.at[base + 1, 0], (z * ROW + other, head),
+                ).start()
+            returned[y, rows] = prefix[y, rows] + factor_of(prefix, y, heights[piece]) * entry
         drain(sends)
-        wait_all(result.at[pl.ds(0, ROW - 1), pl.ds(0, USED)], a_send.at[base + 1])
-        arrive(base + 1, returned, USED)
+        whole = pl.ds(0, USED)
+        wait_all(result.at[pl.ds(0, ROW - 1), whole], a_send.at[base + 1])
+        wait_all(returned.at[pl.ds(0, ROW - 1), whole], a_recv.at[base + 1, 0])
 
     across(0, up, up_in, USED + 1)
 
@@ -418,7 +429,7 @@
         + [square_f] * 2
         + scan * 2
         + [pltpu.VMEM((8, TOK), F32), pltpu.VMEM((HEAD_DEVS, 8, TOK), F32)]
-        + [dma((4,)), dma((4,)), dma((4, 3)), dma((4, 3)), dma, dma],
+        + [dma((4,)), dma((4, 2)), dma((4, 3)), dma((4, 3)), dma, dma],
         compiler_params=pltpu.CompilerParams(
             collective_id=0, has_side_effects=True, vmem_limit_bytes=32 << 20
         ),

time: 53.9 us -> 53 us (0.983)
  Pallas kernels: 52.9 us -> 51.7 us
    pallas_call x1, Pallas kernels: 52.2 us -> 50.9 us  [local(): pl.pallas_call(kernel, out_shape=[result] * 4, in_specs=[hbm] * 6, out_sp...]
where the time goes in v6:
time: 53 us; the launch traced here: 52.3 us
  Pallas kernels  51.7 us (98%)
  between operations  0.64 us (1%)
    pallas_call x1, Pallas kernels, local(): pl.pallas_call(kernel, out_shape=[result] * 4, in_specs=[hbm] * 6, out_sp...  50.9 us

profile of v6, /device:TPU:6, one launch (start us, length us, event | category | flops | bytes accessed | tf_op | source)
XLA Modules:
  0.0 52.3 jit_solution(1721949608276927511)
XLA Ops:
  0.6 50.9 %shard_map.93 = (bf16[128,384]{1,0:T(8,128)(2,1)S(1)}, bf16[128,384]{1,0:T(8,128)(2,1)S(1)}, bf16[128,384]{1,0:T(8,128)(2,1)S(1)}, bf16[128,384]{1,0:T(8,128)(2,1)S(1)}) custom-call(bf16[128,384]{1,0:T(8,128)(2,1)} %q_hbm.1, bf16[128,384]{1,0:T(8,128)(2,1)} %k_hbm.1, bf16[128,384]{1,0:T(8,128)(2,1)} %v_hbm.1, bf16[128,384]{1,0:T(8,128)(2,1)} %g_hbm.1, ...), custom_call_target="tpu_custom_call" | custom-call | tf_op jit(solution)/shard_map/pallas_call | solution.py:419
  51.6 0.8 %shard_map.94 = (bf16[128,384]{1,0:T(8,128)(2,1)}, bf16[128,384]{1,0:T(8,128)(2,1)}, bf16[128,384]{1,0:T(8,128)(2,1)}, bf16[128,384]{1,0:T(8,128)(2,1)}) custom-call(bf16[128,384]{1,0:T(8,128)(2,1)S(1)} %get-tuple-element.8.refs_0_, bf16[128,384]{1,0:T(8,128)(2,1)S(1)} %get-tuple-element.9.refs_1_, bf16[128,384]{1,0:T(8,128)(2,1)S(1)} %get-tuple-element.10.refs_2_, ...), custom_call_target="tpu_custom_call" | custom-call | tf_op jit(solution)/shard_map/pallas_call | solution.py:439

commit v7 on v6

--- a/solution.py
+++ b/solution.py
@@ -15,6 +15,7 @@
 HEAD_DEVS = 8
 PART = 40
 USED = 36
+SPLIT = 4
 CUT = 24
 ORDER = (4, 3, 5, 2, 6, 1, 7)
 EPS = 1e-05
@@ -69,7 +70,7 @@
         return lax.rem(z + step + ROWS, ROWS) * ROW + y
 
     barrier = pltpu.get_barrier_semaphore()
-    for step in range(1, ROW):
+    for step in ORDER:
         pl.semaphore_signal(
             barrier, inc=1, device_id=(z * ROW + lax.rem(y + step, ROW), head), device_id_type=MESH
         )
@@ -87,12 +88,17 @@
     loads = [
         pltpu.make_async_copy(src, dst, in_sem.at[n])
         for n, (src, dst) in enumerate((
-            (ld_hbm, ld_ref), (doc_hbm, doc_ref), (k_hbm, k_ref),
-            (v_hbm, v_ref), (q_hbm, q_ref), (g_hbm, g_ref),
+            (ld_hbm, ld_ref), (doc_hbm.at[pl.ds(ctx, 1)], doc_ref.at[pl.ds(1, 1)]),
+            (k_hbm, k_ref), (v_hbm, v_ref), (q_hbm, q_ref), (g_hbm, g_ref),
+            (doc_hbm.at[pl.ds(jnp.maximum(ctx - 1, 0), 1)], doc_ref.at[pl.ds(0, 1)]),
         ))
     ]
-    for load in loads:
-        load.start()
+    for n in (0, 1, 6):
+        loads[n].start()
+    for n, (src, dst) in enumerate(((k_hbm, k_ref), (v_hbm, v_ref), (q_hbm, q_ref), (g_hbm, g_ref))):
+        for cut in range(SPLIT):
+            rows = pl.ds(TOK // SPLIT * cut, TOK // SPLIT)
+            pltpu.make_async_copy(src.at[rows], dst.at[rows], in_sem.at[n + 2]).start()
 
     lane = lax.broadcasted_iota(jnp.int32, (TOK, TOK), 1)
     sub = lax.broadcasted_iota(jnp.int32, (TOK, TOK), 0)
@@ -124,22 +130,19 @@
 
     loads[0].wait()
     loads[1].wait()
+    loads[6].wait()
     upper = (sub <= lane).astype(F32)
     sums = lax.dot_general(
         ld_ref[...], upper, (((1,), (0,)), ((), ())),
         precision=lax.Precision.HIGHEST, preferred_element_type=F32,
     )
-    doc_row = doc_ref[pl.ds(ctx, 1), :].astype(F32)
-    earlier = doc_ref[pl.ds(jnp.maximum(ctx - 1, 0), 1), :].astype(F32)[:, TOK - 1 : TOK]
+    doc_row = doc_ref[1:2, :].astype(F32)
+    earlier = doc_ref[0:1, TOK - 1 : TOK].astype(F32)
     before = jnp.where(ctx > 0, earlier, -1.0)
     last = doc_row[:, TOK - 1 : TOK]
     enter_row = (doc_row == before).astype(F32)
     leave_row = (doc_row == last).astype(F32)
     through = (last == before).astype(F32)
-    doc_col = spread(doc_row)
-    inside = (sub >= lane) & (doc_col == doc_row)
-    enter_col = (doc_col == before).astype(F32)
-    leave_col = (doc_col == last).astype(F32)
 
     def pack(state, decay, slot, dest):
         tail = state[72:96]
@@ -298,6 +301,11 @@
 
     across(0, up, up_in, USED + 1)
 
+
+    doc_col = spread(doc_row)
+    inside = (sub >= lane) & (doc_col == doc_row)
+    enter_col = (doc_col == before).astype(F32)
+    leave_col = (doc_col == last).astype(F32)
     loads[4].wait()
     loads[5].wait()
     q_heads = heads_of(q_ref)
@@ -336,7 +344,7 @@
     small = lax.broadcasted_iota(jnp.int32, (8, TOK), 0)
     tile = jnp.where(small == 0, square_row, dot_row)
     hsend[...] = tile
-    for step in range(1, HEAD_DEVS):
+    for step in (4, 5, 3, 6, 2, 7, 1):
         other = lax.rem(head + step, HEAD_DEVS)
         copy = remote(hsend.at[pl.ds(0, 2)], hrecv.at[head, pl.ds(0, 2)], h_send, h_recv, (ctx, other))
         copy.start()
@@ -394,8 +402,10 @@
 def write(*refs):
     srcs, dsts, sem = refs[0:4], refs[4:8], refs[8]
     copies = [pltpu.make_async_copy(a, b, sem.at[n]) for n, (a, b) in enumerate(zip(srcs, dsts))]
-    for copy in copies:
-        copy.start()
+    for cut in range(SPLIT):
+        rows = pl.ds(TOK // SPLIT * cut, TOK // SPLIT)
+        for n, (a, b) in enumerate(zip(srcs, dsts)):
+            pltpu.make_async_copy(a.at[rows], b.at[rows], sem.at[n]).start()
     for copy in copies:
         copy.wait()
 
@@ -422,7 +432,7 @@
         in_specs=[hbm] * 6,
         out_specs=[vmem] * 4,
         scratch_shapes=[pltpu.VMEM((TOK, WIDTH), BF16)] * 4
-        + [pltpu.VMEM((HEADS, TOK), F32), pltpu.VMEM((ROW * ROWS, TOK), jnp.int32), dma((6,))]
+        + [pltpu.VMEM((HEADS, TOK), F32), pltpu.VMEM((8, TOK), jnp.int32), dma((7,))]
         + [square_bf] * 4
         + [square_f] * 6
         + [square_bf] * 4

time: 53 us -> 52.9 us (level)
  no operation moved by 1% of the time
where the time goes in v7:
time: 52.9 us; the launch traced here: 52.4 us
  Pallas kernels  51.7 us (98%)
  between operations  0.64 us (1%)
    pallas_call x1, Pallas kernels, local(): pl.pallas_call(kernel, out_shape=[result] * 4, in_specs=[hbm] * 6, out_sp...  50.9 us

profile of v7, /device:TPU:6, one launch (start us, length us, event | category | flops | bytes accessed | tf_op | source)
XLA Modules:
  0.0 52.4 jit_solution(2153247937123814560)
XLA Ops:
  0.6 50.9 %shard_map.93 = (bf16[128,384]{1,0:T(8,128)(2,1)S(1)}, bf16[128,384]{1,0:T(8,128)(2,1)S(1)}, bf16[128,384]{1,0:T(8,128)(2,1)S(1)}, bf16[128,384]{1,0:T(8,128)(2,1)S(1)}) custom-call(bf16[128,384]{1,0:T(8,128)(2,1)} %q_hbm.1, bf16[128,384]{1,0:T(8,128)(2,1)} %k_hbm.1, bf16[128,384]{1,0:T(8,128)(2,1)} %v_hbm.1, bf16[128,384]{1,0:T(8,128)(2,1)} %g_hbm.1, ...), custom_call_target="tpu_custom_call" | custom-call | tf_op jit(solution)/shard_map/pallas_call | solution.py:429
  51.6 0.8 %shard_map.94 = (bf16[128,384]{1,0:T(8,128)(2,1)}, bf16[128,384]{1,0:T(8,128)(2,1)}, bf16[128,384]{1,0:T(8,128)(2,1)}, bf16[128,384]{1,0:T(8,128)(2,1)}) custom-call(bf16[128,384]{1,0:T(8,128)(2,1)S(1)} %get-tuple-element.8.refs_0_, bf16[128,384]{1,0:T(8,128)(2,1)S(1)} %get-tuple-element.9.refs_1_, bf16[128,384]{1,0:T(8,128)(2,1)S(1)} %get-tuple-element.10.refs_2_, ...), custom_call_target="tpu_custom_call" | custom-call | tf_op jit(solution)/shard_map/pallas_call | solution.py:449

commit v8 on v7

--- a/solution.py
+++ b/solution.py
@@ -55,7 +55,7 @@
     att_ref, dq_ref, dk_ref, dv_ref,
     q_ref, k_ref, v_ref, g_ref, ld_ref, doc_ref, in_sem,
     qh, kh, vh, gh, qt, within, score, ent, leave, out, state_hi, state_lo,
-    out_hi, out_lo, dkl, dvl,
+    joint, out_lo, dkl, dvl,
     up, up_in, part, back, back_in, zout, zin,
     upb, upb_in, partb, backb, backb_in, zoutb, zinb,
     hsend, hrecv,
@@ -351,7 +351,8 @@
     hrecv[pl.ds(head, 1)] = tile[None]
     for h in range(HEADS):
         pair = split(out[h])
-        out_hi[h] = pair[0]
+        joint[h, 0:TOK] = gh[h]
+        joint[h, TOK : 2 * TOK] = pair[0]
         out_lo[h] = pair[1]
     wait_all(hrecv.at[pl.ds(0, HEAD_DEVS - 1), pl.ds(0, 2)], h_send)
     wait_all(hrecv.at[pl.ds(0, HEAD_DEVS - 1), pl.ds(0, 2)], h_recv)
@@ -362,9 +363,8 @@
     drift = rscale * rscale * rscale * total[1:2] / FULL
 
     for h in range(HEADS):
-        near = split(qt[h] * rscale)
-        far = split(qt[h] * drift)
-        pulled = two(nn, near, gh[h]) - three(nn, far, (out_hi[h], out_lo[h]))
+        left = split(jnp.concatenate([qt[h] * rscale, qt[h] * -drift], axis=1))
+        pulled = two(nn, left, joint[h]) + nn(left[0][:, TOK : 2 * TOK], out_lo[h])
         pack(pulled, passing[h], 2 * h, upb)
 
     across(2, upb, upb_in, USED)
@@ -435,7 +435,8 @@
         + [pltpu.VMEM((HEADS, TOK), F32), pltpu.VMEM((8, TOK), jnp.int32), dma((7,))]
         + [square_bf] * 4
         + [square_f] * 6
-        + [square_bf] * 4
+        + [square_bf] * 2
+        + [pltpu.VMEM((HEADS, 2 * TOK, TOK), BF16), square_bf]
         + [square_f] * 2
         + scan * 2
         + [pltpu.VMEM((8, TOK), F32), pltpu.VMEM((HEAD_DEVS, 8, TOK), F32)]

time: 52.9 us -> 52.8 us (level)
  no operation moved by 1% of the time
where the time goes in v8:
time: 52.8 us; the launch traced here: 52.3 us
  Pallas kernels  51.7 us (98%)
  between operations  0.64 us (1%)
    pallas_call x1, Pallas kernels, local(): pl.pallas_call(kernel, out_shape=[result] * 4, in_specs=[hbm] * 6, out_sp...  50.9 us

profile of v8, /device:TPU:6, one launch (start us, length us, event | category | flops | bytes accessed | tf_op | source)
XLA Modules:
  0.0 52.3 jit_solution(2520843324120341625)
XLA Ops:
  0.6 50.9 %shard_map.93 = (bf16[128,384]{1,0:T(8,128)(2,1)S(1)}, bf16[128,384]{1,0:T(8,128)(2,1)S(1)}, bf16[128,384]{1,0:T(8,128)(2,1)S(1)}, bf16[128,384]{1,0:T(8,128)(2,1)S(1)}) custom-call(bf16[128,384]{1,0:T(8,128)(2,1)} %q_hbm.1, bf16[128,384]{1,0:T(8,128)(2,1)} %k_hbm.1, bf16[128,384]{1,0:T(8,128)(2,1)} %v_hbm.1, bf16[128,384]{1,0:T(8,128)(2,1)} %g_hbm.1, ...), custom_call_target="tpu_custom_call" | custom-call | tf_op jit(solution)/shard_map/pallas_call | solution.py:429
  51.5 0.8 %shard_map.94 = (bf16[128,384]{1,0:T(8,128)(2,1)}, bf16[128,384]{1,0:T(8,128)(2,1)}, bf16[128,384]{1,0:T(8,128)(2,1)}, bf16[128,384]{1,0:T(8,128)(2,1)}) custom-call(bf16[128,384]{1,0:T(8,128)(2,1)S(1)} %get-tuple-element.8.refs_0_, bf16[128,384]{1,0:T(8,128)(2,1)S(1)} %get-tuple-element.9.refs_1_, bf16[128,384]{1,0:T(8,128)(2,1)S(1)} %get-tuple-element.10.refs_2_, ...), custom_call_target="tpu_custom_call" | custom-call | tf_op jit(solution)/shard_map/pallas_call | solution.py:450
